TPU v7x, 128 devices: a whole 4x4x4 slice. The times are simulated.
128 devices in a mesh: tile: 32 (over x, z, core), dp: 4 (over y).
Axes of the slice: x: 4, y: 4, z: 4, core: 2. Of those that a mesh axis runs over, the one named last changes fastest.
Arguments:
- fields: bfloat16 [4, 64, 64, 64, 128], P('dp', 'tile'), may hold values from -6 to 6
- cotangent: bfloat16 [4, 64, 64, 64, 128], P('dp', 'tile'), may hold values from -6 to 6
- is_ocean: int32 [64], P('tile'), may hold values from 0 to 1, as said below
- neighbours: int32 [64, 8], P('tile'), may hold values from -1 to 63, as said below
- kernel: float32 [7, 7, 128], replicated, may hold values from -0.875 to 0.875
- conv_bias: float32 [128], replicated, may hold values from -3 to 3
- ln_gain: float32 [128], replicated, may hold values from 0.25 to 1.75
- ln_bias: float32 [128], replicated, may hold values from -3 to 3
- w_up: bfloat16 [128, 512], replicated, may hold values from -0.5 to 0.5
- up_bias: float32 [512], replicated, may hold values from -3 to 3
- w_down: bfloat16 [512, 128], replicated, may hold values from -0.25 to 0.25
- down_bias: float32 [128], replicated, may hold values from -3 to 3
- layer_scale: float32 [128], replicated, may hold values from 0.3 to 1
Outputs:
- grad_fields: bfloat16 [4, 64, 64, 64, 128], P('dp', 'tile')
- g_kernel: float32 [7, 7, 128], replicated
- g_conv_bias: float32 [128], replicated
- g_ln_gain: float32 [128], replicated
- g_ln_bias: float32 [128], replicated
- g_w_up: float32 [128, 512], replicated
- g_up_bias: float32 [512], replicated
- g_w_down: float32 [512, 128], replicated
- g_down_bias: float32 [128], replicated
- g_layer_scale: float32 [128], replicated
Inputs may be any that keep to these rules, and one draw needn't show every extreme that they name: `is_ocean`: slots follow a serpentine curve through the columns of a grid of 8 x 8 tiles, alternating direction from column to column; tiles of the first and last grid rows are ocean. Entry k of slot s names the slot of the tile adjacent in direction k (north, south, west, east, north-west, north-east, south-west, south-east), or -1 where that tile is land or outside the grid or slot s is land; the relation is symmetric; the north and south neighbours are slot s - 1 or s + 1, and every neighbour lies within 15 slots of s.
All inputs are finite; a program needn't handle non-finite values.
Results may differ from a plain program's by a relative error of at most 0.0071.
Values may be sent and summed in bfloat16 or wider, within the bound.
No kernel may reach another device: no remote copies, remote signals or barrier semaphores. Data moves between devices by JAX's collectives and lax.ppermute only.
A program may use at most 128 MiB of HBM per device.

v0:
```python
from functools import partial
import math
import jax
import jax.numpy as jnp
from jax import lax
from jax.sharding import PartitionSpec as P

TROWS = 8
EPSILON = 1e-06


def passed_along(value, axis, by):
    devices = lax.axis_size(axis)
    pairs = [(i, i + by) for i in range(devices) if 0 <= i + by < devices]
    return lax.ppermute(value, axis, pairs)


def rims_of(tile_block, rim_depth):
    extent = tile_block.shape[0]
    top_band = tile_block[:rim_depth]
    bottom = tile_block[extent - rim_depth :]
    left_band = jnp.transpose(tile_block[:, :rim_depth], (1, 0, 2))
    right_band = jnp.transpose(tile_block[:, extent - rim_depth :], (1, 0, 2))
    return jnp.stack([top_band, bottom, left_band, right_band], 0)


def assemble(own_tile, picked, valid_flags, first_layer, rim_depth):
    extent = own_tile.shape[0]

    def rim_piece(direction, which_strip):
        stripe = picked[direction][which_strip, first_layer : first_layer + rim_depth]
        return stripe * valid_flags[direction].astype(own_tile.dtype)

    north_rim = rim_piece(0, 1)
    south_rim = rim_piece(1, 0)
    west_rim = jnp.transpose(rim_piece(2, 1), (1, 0, 2))
    east_rim = jnp.transpose(rim_piece(3, 0), (1, 0, 2))
    north_west = jnp.transpose(rim_piece(4, 1)[:, extent - rim_depth :], (1, 0, 2))
    north_east = jnp.transpose(rim_piece(5, 0)[:, extent - rim_depth :], (1, 0, 2))
    south_west = jnp.transpose(rim_piece(6, 1)[:, :rim_depth], (1, 0, 2))
    south_east = jnp.transpose(rim_piece(7, 0)[:, :rim_depth], (1, 0, 2))
    top_band = jnp.concatenate([north_west, north_rim, north_east], 1)
    middle = jnp.concatenate([west_rim, own_tile, east_rim], 1)
    bottom = jnp.concatenate([south_west, south_rim, south_east], 1)
    return jnp.concatenate([top_band, middle, bottom], 0)


def depthwise(padded, kernel, extent):
    running_sum = jnp.zeros((extent, extent, padded.shape[2]), jnp.float32)
    for lag_row in range(7):
        for lag_col in range(7):
            window = padded[lag_row : lag_row + extent, lag_col : lag_col + extent].astype(
                jnp.float32
            )
            running_sum = running_sum + window * kernel[lag_row, lag_col]
    return running_sum


def transposed(grad_padded, kernel, extent):
    running_sum = jnp.zeros((extent, extent, grad_padded.shape[2]), jnp.float32)
    for lag_row in range(7):
        for lag_col in range(7):
            window = grad_padded[
                6 - lag_row : 6 - lag_row + extent, 6 - lag_col : 6 - lag_col + extent
            ].astype(jnp.float32)
            running_sum = running_sum + window * kernel[lag_row, lag_col]
    return running_sum


def kernel_terms(grad_tile, padded, extent):
    grad_values = grad_tile.astype(jnp.float32)
    stacked = []
    for lag_row in range(7):
        line_terms = []
        for lag_col in range(7):
            window = padded[lag_row : lag_row + extent, lag_col : lag_col + extent].astype(
                jnp.float32
            )
            line_terms.append(jnp.sum(grad_values * window, axis=(0, 1)))
        stacked.append(jnp.stack(line_terms, 0))
    return jnp.stack(stacked, 0)


def gelu_tanh(values):
    return jax.nn.gelu(values, approximate=True)


def contract_last(left_rows, right_matrix):
    return lax.dot_general(
        left_rows, right_matrix, (((1,), (1,)), ((), ())), preferred_element_type=jnp.float32
    )


def contract_first(left_rows, right_rows):
    return lax.dot_general(
        left_rows, right_rows, (((0,), (0,)), ((), ())), preferred_element_type=jnp.float32
    )


def layer_rows(
    conv_rows, cot_rows, ln_gain, ln_bias, w_up, up_bias, w_down, down_bias, layer_scale
):
    mean_value = jnp.mean(conv_rows, -1, keepdims=True)
    centred = conv_rows - mean_value
    variance = jnp.mean(centred * centred, -1, keepdims=True)
    inverse_scale = lax.rsqrt(variance + EPSILON)
    normed = centred * inverse_scale
    scaled = (normed * ln_gain + ln_bias).astype(jnp.bfloat16)
    hidden_sum = jnp.dot(scaled, w_up, preferred_element_type=jnp.float32) + up_bias
    activation = gelu_tanh(hidden_sum).astype(jnp.bfloat16)
    mixed = jnp.dot(activation, w_down, preferred_element_type=jnp.float32) + down_bias
    grad_mixed = (cot_rows * layer_scale).astype(jnp.bfloat16)
    grad_act = contract_last(grad_mixed, w_down)
    pullback = jax.vjp(gelu_tanh, hidden_sum)[1]
    grad_pre = pullback(grad_act)[0].astype(jnp.bfloat16)
    grad_scaled = contract_last(grad_pre, w_up)
    grad_normed = grad_scaled * ln_gain
    grad_conv = inverse_scale * (
        grad_normed
        - jnp.mean(grad_normed, -1, keepdims=True)
        - normed * jnp.mean(grad_normed * normed, -1, keepdims=True)
    )
    return (
        grad_conv.astype(jnp.bfloat16),
        mixed,
        grad_mixed,
        activation,
        grad_pre,
        scaled,
        grad_scaled,
        normed,
    )


def row_terms(
    cot_rows, mixed, grad_mixed, activation, grad_pre, scaled, grad_scaled, normed, grad_conv
):
    return (
        jnp.sum(grad_conv.astype(jnp.float32), 0),
        jnp.sum(grad_scaled * normed, 0),
        jnp.sum(grad_scaled, 0),
        contract_first(scaled, grad_pre),
        jnp.sum(grad_pre.astype(jnp.float32), 0),
        contract_first(activation, grad_mixed),
        jnp.sum(grad_mixed.astype(jnp.float32), 0),
        jnp.sum(cot_rows * mixed, 0),
    )


def local(
    fields,
    cotangent,
    is_ocean,
    neighbours,
    kernel,
    conv_bias,
    ln_gain,
    ln_bias,
    w_up,
    up_bias,
    w_down,
    down_bias,
    layer_scale,
):
    samples, slot_count, extent, channels = (
        fields.shape[0],
        fields.shape[1],
        fields.shape[2],
        fields.shape[4],
    )
    hidden_width = w_up.shape[1]
    tile_count = lax.axis_size("tile")
    reach_span = min((2 * TROWS + slot_count - 2) // slot_count, tile_count - 1)
    position = lax.axis_index("tile")
    vert_base = (position - 1) * slot_count
    side_base = (position - reach_span) * slot_count
    layer_params = (ln_gain, ln_bias, w_up, up_bias, w_down, down_bias, layer_scale)
    zero_terms = (
        jnp.zeros((7, 7, channels), jnp.float32),
        jnp.zeros((channels,), jnp.float32),
        jnp.zeros((channels,), jnp.float32),
        jnp.zeros((channels,), jnp.float32),
        jnp.zeros((channels, hidden_width), jnp.float32),
        jnp.zeros((hidden_width,), jnp.float32),
        jnp.zeros((hidden_width, channels), jnp.float32),
        jnp.zeros((channels,), jnp.float32),
        jnp.zeros((channels,), jnp.float32),
    )

    def collect(rim_set):
        adjacent = {}
        for offset in (1, -1):
            adjacent[offset] = passed_along(rim_set, "tile", offset)
        vertical = jnp.concatenate([adjacent[1], rim_set, adjacent[-1]], 1)
        distant = {}
        for distance in range(2, reach_span + 1):
            for offset in (distance, -distance):
                distant[offset] = passed_along(rim_set, "tile", offset)[:, :, 2:4]
        below_list = [distant[distance] for distance in range(reach_span, 1, -1)]
        above_list = [distant[-distance] for distance in range(2, reach_span + 1)]
        middle_list = [adjacent[1][:, :, 2:4], rim_set[:, :, 2:4], adjacent[-1][:, :, 2:4]]
        sideways = jnp.concatenate(below_list + middle_list + above_list, 1)
        bases = jnp.zeros((6,), jnp.int32) + side_base
        return (vertical, sideways, bases)

    def fetch_rims(vertical, sideways, bases, slot_ids):
        upright = jnp.clip(slot_ids[:2] - vert_base, 0, vertical.shape[0] - 1)
        lateral = jnp.clip(slot_ids[2:] - bases, 0, sideways.shape[0] - 1)
        picked = [vertical[upright[0]], vertical[upright[1]]]
        picked = picked + [sideways[lateral[slot_pick]] for slot_pick in range(6)]
        return (picked, slot_ids >= 0)

    grad_sums = zero_terms
    rims_x = jax.vmap(jax.vmap(partial(rims_of, rim_depth=3)))(fields)
    vertical_x, sideways_x, bases_x = collect(rims_x)
    sample = 0
    tile_stack = fields[sample]
    cot_stack = cotangent[sample]

    def first_work(slot_id):
        picked, valid_flags = fetch_rims(
            vertical_x[sample], sideways_x[sample], bases_x, neighbours[slot_id]
        )
        padded = assemble(tile_stack[slot_id], picked, valid_flags, 0, 3)
        conv_out = depthwise(padded, kernel, extent) + conv_bias
        cot_rows = cot_stack[slot_id].astype(jnp.float32).reshape(-1, channels)
        layer_parts = layer_rows(conv_out.reshape(-1, channels), cot_rows, *layer_params)
        grad_tile = layer_parts[0].reshape(extent, extent, channels)
        weight_terms = (kernel_terms(grad_tile, padded, extent),) + row_terms(
            cot_rows, *layer_parts[1:], layer_parts[0]
        )
        keep_flag = (is_ocean[slot_id] > 0).astype(jnp.float32)
        return (grad_tile, tuple((keep_flag * term for term in weight_terms)))

    def first_step(running, slot_id):
        grad_tile, weight_terms = first_work(slot_id)
        return (tuple((total + term for total, term in zip(running, weight_terms))), grad_tile)

    grad_sums, sample_grads = lax.scan(first_step, grad_sums, jnp.arange(slot_count))
    grad_tiles = [sample_grads]
    grad_stack = jnp.stack(grad_tiles, 0)
    rims_g = jax.vmap(jax.vmap(partial(rims_of, rim_depth=3)))(grad_stack)
    vertical_g, sideways_g, bases_g = collect(rims_g)
    sample = 0
    cot_stack = cotangent[sample]

    def second_step(slot_id):
        picked, valid_flags = fetch_rims(
            vertical_g[sample], sideways_g[sample], bases_g, neighbours[slot_id]
        )
        grad_padded = assemble(grad_stack[sample, slot_id], picked, valid_flags, 0, 3)
        result = cot_stack[slot_id].astype(jnp.float32) + transposed(grad_padded, kernel, extent)
        keep_flag = (is_ocean[slot_id] > 0).astype(jnp.float32)
        return (result * keep_flag).astype(jnp.bfloat16)

    outputs = [lax.map(second_step, jnp.arange(slot_count))]
    summed = lax.psum(
        (
            grad_sums[0],
            grad_sums[1],
            grad_sums[2],
            grad_sums[3],
            grad_sums[4],
            grad_sums[5],
            grad_sums[6],
            grad_sums[7],
            grad_sums[8],
        ),
        ("tile", "dp"),
    )
    grad_scale = 1.0 / math.sqrt(
        samples * lax.axis_size("dp") * slot_count * tile_count * extent * extent
    )
    return (
        jnp.stack(outputs, 0),
        summed[0] * grad_scale,
        summed[1] * grad_scale,
        summed[2] * grad_scale,
        summed[3] * grad_scale,
        summed[4] * grad_scale,
        summed[5] * grad_scale,
        summed[6] * grad_scale,
        summed[7] * grad_scale,
        summed[8] * grad_scale,
    )


def solution(mesh):
    placed = (
        P("dp", "tile", None, None, None),
        P("dp", "tile", None, None, None),
        P("tile"),
        P("tile", None),
        P(),
        P(),
        P(),
        P(),
        P(),
        P(),
        P(),
        P(),
        P(),
    )
    return jax.shard_map(
        local,
        mesh=mesh,
        in_specs=placed,
        out_specs=(P("dp", "tile", None, None, None), P(), P(), P(), P(), P(), P(), P(), P(), P()),
        check_vma=False,
    )
```

profile of v0, /device:TPU:1, one launch (start us, length us, event | category | flops | bytes accessed | tf_op | source)
XLA Modules:
  0.0 865.7 jit_solution(16494934024993436842)
XLA Ops:
  9.4 4.0 collective-permute-start
  13.4 4.0 collective-permute-start.1
  17.4 5.7 collective-permute-start.2
  23.0 2.0 collective-permute-start.3
  25.1 5.1 collective-permute-start.4
  30.3 2.6 collective-permute-start.5
  32.9 2.7 collective-permute-start.6
  35.7 13.1 %collective-permute-done.2 = bf16[1,2,4,3,64,128]{5,4,3,2,1,0:T(8,128)(2,1)S(1)} collective-permute-done((bf16[1,2,4,3,64,128]{5,4,3,2,1,0:T(8,128)(2,1)S(1)}, bf16[1,2,4,3,64,128]{5,4,3,2,1,0:T(8,128)(2,1)S(1)}, u32[]{:S(2)}, u32[]{:S(2)}) %collective-permute-start.2) | collective-permute-done | bytes 393248 | tf_op jit(solution)/shard_map/ppermute | solution.py:15
  48.8 1.9 collective-permute-start.7
  50.7 3.1 collective-permute-done.3
  53.8 1.9 collective-permute-start.8
  61.6 4.2 collective-permute-done.8
  73.0 4.9 collective-permute-done.11
  77.9 10.7 %collective-permute-done.12 = bf16[1,2,4,3,64,128]{5,4,3,2,1,0:T(8,128)(2,1)S(1)} collective-permute-done((bf16[1,2,4,3,64,128]{5,4,3,2,1,0:T(8,128)(2,1)S(1)}, bf16[1,2,4,3,64,128]{5,4,3,2,1,0:T(8,128)(2,1)S(1)}, u32[]{:S(2)}, u32[]{:S(2)}) %collective-permute-start.12) | collective-permute-done | bytes 393248 | tf_op jit(solution)/shard_map/ppermute | solution.py:15
  88.6 8.4 collective-permute-done.13
  97.0 22.3 %collective-permute-done.14 = bf16[1,2,4,3,64,128]{5,4,3,2,1,0:T(8,128)(2,1)S(1)} collective-permute-done((bf16[1,2,4,3,64,128]{5,4,3,2,1,0:T(8,128)(2,1)S(1)}, bf16[1,2,4,3,64,128]{5,4,3,2,1,0:T(8,128)(2,1)S(1)}, u32[]{:S(2)}, u32[]{:S(2)}) %collective-permute-start.14) | collective-permute-done | bytes 393248 | tf_op jit(solution)/shard_map/ppermute | solution.py:15
  121.0 6.8 copy.25
  130.9 242.7 %while.43 = (s32[]{:T(128)}, f32[7,7,128]{2,1,0:T(8,128)}, f32[128]{0:T(128)}, f32[128]{0:T(128)}, f32[128]{0:T(128)}, /*index=5*/f32[128,512]{1,0:T(8,128)}, f3...) while((s32[]{:T(128)}, f32[7,7,128]{2,1,0:T(8,128)}, ...), condition=%wide.region_60.61_spmd.clone, body=%wide.region_0.60_spmd.clone.sunk | while | flops 3501007360 | bytes 273028160 | solution.py:239
  174.1 3.2 maximum_maximum_fusion.7
  177.4 16.3 %fusion.232 = (f32[64,64]{1,0:T(8,128)S(1)}, f32[64,64,128]{2,1,0:T(8,128)S(1)}) fusion(f32[128]{0:T(128)S(1)} %get-tuple-element.1736, f32[128]{0:T(128)S(1)} %get-tuple-element.1527, bf16[67,70,128]{2,1,0:T(8,128)(2,1)S(1)} %get-tuple-element.1526, f32[128]{0:T(128)S(1)} %get-tuple-element.1528, f32[128]{0:T(128)S(1)} %get-tuple-element.1529, ...), kind=kLoop, calls=%fused_computation.494.clone.1 | loop fusion | flops 87027712 | bytes 47326208 | tf_op jit(solution)/shard_map/while/body/eval_jaxpr/reduce_sum | solution.py:103
  196.5 3.7 add_convert_fusion.2
  200.2 3.3 multiply_convert_fusion.5
  203.8 7.3 convert_reduce_fusion.6
  211.0 3.0 multiply_reduce_fusion.7
  214.1 9.7 %fusion.234 = (f32[128]{0:T(128)}, f32[128]{0:T(128)}, f32[128]{0:T(128)}, f32[128]{0:T(128)}, f32[128]{0:T(128)}, /*index=5*/f32[128]{0:T(128)}, f32[128]{0:T(1...) fusion(bf16[67,70,128]{2,1,0:T(8,128)(2,1)S(1)} %get-tuple-elem, ...), kind=kLoop, calls=%fused_computation.301.clone.1 | loop fusion | flops 33027840 | bytes 24192512 | tf_op jit(solution)/shard_map/while/body/eval_jaxpr/reduce_sum | solution.py:79
  224.4 2.4 fusion.241
  228.7 4.0 fusion.239
  237.3 8.7 %fusion.235 = (f32[128]{0:T(128)}, f32[128]{0:T(128)}, f32[128]{0:T(128)}, f32[128]{0:T(128)}, f32[128]{0:T(128)}, /*index=5*/f32[128]{0:T(128)}, f32[128]{0:T(1...) fusion(bf16[67,70,128]{2,1,0:T(8,128)(2,1)S(1)} %get-tuple-element.1526, ...), kind=kLoop, calls=%fused_computation.283.clone.1 | loop fusion | flops 28834304 | bytes 8493056 | tf_op jit(solution)/shard_map/while/body/eval_jaxpr/reduce_sum | solution.py:79
  247.5 5.2 fusion.236
  254.9 4.3 fusion.240
  288.2 3.2 maximum_maximum_fusion.7
  291.5 16.3 %fusion.232 = (f32[64,64]{1,0:T(8,128)S(1)}, f32[64,64,128]{2,1,0:T(8,128)S(1)}) fusion(f32[128]{0:T(128)S(1)} %get-tuple-element.1736, f32[128]{0:T(128)S(1)} %get-tuple-element.1527, bf16[67,70,128]{2,1,0:T(8,128)(2,1)S(1)} %get-tuple-element.1526, f32[128]{0:T(128)S(1)} %get-tuple-element.1528, f32[128]{0:T(128)S(1)} %get-tuple-element.1529, ...), kind=kLoop, calls=%fused_computation.494.clone.1 | loop fusion | flops 87027712 | bytes 47326208 | tf_op jit(solution)/shard_map/while/body/eval_jaxpr/reduce_sum | solution.py:103
  310.5 3.7 add_convert_fusion.2
  314.3 3.3 multiply_convert_fusion.5
  317.8 7.3 convert_reduce_fusion.6
  325.1 3.0 multiply_reduce_fusion.7
  328.1 9.7 %fusion.234 = (f32[128]{0:T(128)}, f32[128]{0:T(128)}, f32[128]{0:T(128)}, f32[128]{0:T(128)}, f32[128]{0:T(128)}, /*index=5*/f32[128]{0:T(128)}, f32[128]{0:T(1...) fusion(bf16[67,70,128]{2,1,0:T(8,128)(2,1)S(1)} %get-tuple-elem, ...), kind=kLoop, calls=%fused_computation.301.clone.1 | loop fusion | flops 33027840 | bytes 24192512 | tf_op jit(solution)/shard_map/while/body/eval_jaxpr/reduce_sum | solution.py:79
  338.5 2.4 fusion.241
  342.8 4.0 fusion.239
  351.3 8.7 %fusion.235 = (f32[128]{0:T(128)}, f32[128]{0:T(128)}, f32[128]{0:T(128)}, f32[128]{0:T(128)}, f32[128]{0:T(128)}, /*index=5*/f32[128]{0:T(128)}, f32[128]{0:T(1...) fusion(bf16[67,70,128]{2,1,0:T(8,128)(2,1)S(1)} %get-tuple-element.1526, ...), kind=kLoop, calls=%fused_computation.283.clone.1 | loop fusion | flops 28834304 | bytes 8493056 | tf_op jit(solution)/shard_map/while/body/eval_jaxpr/reduce_sum | solution.py:79
  361.5 5.2 fusion.236
  369.0 4.3 fusion.240
  376.5 6.5 collective-permute-start.23
  383.0 1.9 collective-permute-start.24
  385.0 4.1 collective-permute-start.16
  389.0 6.0 collective-permute-start.17
  396.4 82.6 %all-reduce = (f32[7,7,128]{2,1,0:T(8,128)S(1)}, f32[128]{0:T(128)S(1)}, f32[128]{0:T(128)S(1)}, f32[128]{0:T(128)S(1)}, f32[512]{0:T(512)S(1)}, /*index=5*/f32[128]{0:T(128)S(1)}, f32[128]{0:T(128)S(1)}) all-reduce(f32[7,7,128]{2,1,0:T(8,128)S(1)} %copy-done.21, ...), channel_id=1, replica_groups=mesh['tile'=32,'dp'=4] {'tile','dp'}, use_global_device_ids=true, to_apply=%region_63.64 | all-reduce | flops 7424 | bytes 59392 | tf_op jit(solution)/shard_map/psum | solution.py:257
  482.8 142.8 %all-reduce.4.cloned.1.call-done = (f32[128,512]{1,0:T(8,128)}, f32[512,128]{1,0:T(8,128)}) async-done(((f32[128,512]{1,0:T(8,128)}, f32[512,128]{1,0:T(8,128)}), (f32[128,512]{1,0:T(8,128)}, f32[512,128]{1,0:T(8,128)})) %all-reduce.4.cloned.1.call-update) | async-done | bytes 524304 | tf_op jit(solution)/shard_map/psum | solution.py:257
  629.0 3.6 collective-permute-start.19
  632.6 2.8 collective-permute-start.20
  636.9 6.0 collective-permute-start.21
  644.0 2.5 collective-permute-start.22
  649.0 34.7 %collective-permute-done.19 = bf16[1,2,4,3,64,128]{5,3,4,1,0,2:T(4,128)(2,1)S(1)} collective-permute-done((bf16[1,2,4,3,64,128]{5,3,4,1,0,2:T(4,128)(2,1)S(1)}, bf16[1,2,4,3,64,128]{5,3,4,1,0,2:T(4,128)(2,1)S(1)}, u32[]{:S(2)}, u32[]{:S(2)}) %collective-permute-start.19) | collective-permute-done | bytes 393248 | tf_op jit(solution)/shard_map/ppermute | solution.py:15
  689.7 1.9 collective-permute-done.25
  693.0 18.9 %collective-permute-done.26 = bf16[1,2,4,3,64,128]{5,3,4,1,0,2:T(4,128)(2,1)S(1)} collective-permute-done((bf16[1,2,4,3,64,128]{5,3,4,1,0,2:T(4,128)(2,1)S(1)}, bf16[1,2,4,3,64,128]{5,3,4,1,0,2:T(4,128)(2,1)S(1)}, u32[]{:S(2)}, u32[]{:S(2)}) %collective-permute-start.26) | collective-permute-done | bytes 393248 | tf_op jit(solution)/shard_map/ppermute | solution.py:15
  713.3 2.3 collective-permute-done.27
  716.0 22.6 %collective-permute-done.30 = bf16[1,2,4,3,64,128]{5,3,4,1,0,2:T(4,128)(2,1)S(1)} collective-permute-done((bf16[1,2,4,3,64,128]{5,3,4,1,0,2:T(4,128)(2,1)S(1)}, bf16[1,2,4,3,64,128]{5,3,4,1,0,2:T(4,128)(2,1)S(1)}, u32[]{:S(2)}, u32[]{:S(2)}) %collective-permute-start.30) | collective-permute-done | bytes 393248 | tf_op jit(solution)/shard_map/ppermute | solution.py:15
  738.7 14.6 %collective-permute-done.31 = bf16[1,2,4,3,64,128]{5,3,4,1,0,2:T(4,128)(2,1)S(1)} collective-permute-done((bf16[1,2,4,3,64,128]{5,3,4,1,0,2:T(4,128)(2,1)S(1)}, bf16[1,2,4,3,64,128]{5,3,4,1,0,2:T(4,128)(2,1)S(1)}, u32[]{:S(2)}, u32[]{:S(2)}) %collective-permute-start.31) | collective-permute-done | bytes 393248 | tf_op jit(solution)/shard_map/ppermute | solution.py:15
  753.4 4.0 copy.28
  759.3 99.1 %while.42 = (s32[]{:T(128)}, bf16[2,64,64,128]{3,2,1,0:T(8,128)(2,1)}, s32[2]{0:T(128)S(1)}, bf16[2,64,64,128]{3,2,1,0:T(8,128)(2,1)S(1)}, s32[2,8]{1,0:T(2,128)...) while((s32[]{:T(128)}, ...), condition=%wide.region_62.63_spmd.clone, body=%wide.region_61.62_spmd.clone.sunk | while | flops 102684736 | bytes 53919052 | solution.py:256
  787.6 3.3 maximum_maximum_fusion.6
  792.3 16.7 %bitcast_dynamic-update-slice_fusion.2 = bf16[2,64,64,128]{3,2,1,0:T(8,128)(2,1)} fusion(bf16[2,64,64,128]{3,2,1,0:T(8,128)(2,1)} %get-tuple-element.1773, s32[]{:T(128)} %get-tuple-element.1772, f32[]{:T(128)} %bitcast.632, f32[128]{0:T(128)S(1)} %get-tuple-element.1390, bf16[67,70,128]{2,1,0:T(8,128)(2,1)S(1)} %get-tuple-element.1421, ...), kind=kLoop, calls=%fused_computation.21.clone.1 | loop fusion | flops 88080384 | bytes 47310340 | tf_op jit(solution)/shard_map/while/body/jit(dynamic_update_index_in_dim)/dynamic_update_slice | solution.py:239
  837.0 3.3 maximum_maximum_fusion.6
  841.7 16.7 %bitcast_dynamic-update-slice_fusion.2 = bf16[2,64,64,128]{3,2,1,0:T(8,128)(2,1)} fusion(bf16[2,64,64,128]{3,2,1,0:T(8,128)(2,1)} %get-tuple-element.1773, s32[]{:T(128)} %get-tuple-element.1772, f32[]{:T(128)} %bitcast.632, f32[128]{0:T(128)S(1)} %get-tuple-element.1390, bf16[67,70,128]{2,1,0:T(8,128)(2,1)S(1)} %get-tuple-element.1421, ...), kind=kLoop, calls=%fused_computation.21.clone.1 | loop fusion | flops 88080384 | bytes 47310340 | tf_op jit(solution)/shard_map/while/body/jit(dynamic_update_index_in_dim)/dynamic_update_slice | solution.py:239
  (494 shorter events, 97.1 us)
Async XLA Ops:
  7.2 618.5 %all-reduce.4.cloned.1.call-start = ((), (), s32[]{:S(2)}) async-start(), calls=%async_computation | async-start | bytes 1048576 | tf_op jit(solution)/shard_map/psum | solution.py:257
  9.4 20.9 %collective-permute-start = (bf16[1,2,4,3,64,128]{5,4,3,2,1,0:T(8,128)(2,1)S(1)}, bf16[1,2,4,3,64,128]{5,4,3,2,1,0:T(8,128)(2,1)S(1)}, u32[]{:S(2)}, u32[]{:S(2)}) collective-permute-start(bf16[1,2,4,3,64,128]{5,4,3,2,1,0:T(8,128)(2,1)S(1)} %maximum_bitcast_fusion.1), channel_id=1, source_target_pairs={{0,32},{4,36},{8,40},{12,44},{16,48},{20,52},{24,56},{28,60},{32,6... | collective-permute-start | bytes 1179656 | tf_op jit(solution)/shard_map/ppermute | solution.py:15
  13.4 19.5 %collective-permute-start.1 = (bf16[1,2,4,3,64,128]{5,4,3,2,1,0:T(8,128)(2,1)S(1)}, bf16[1,2,4,3,64,128]{5,4,3,2,1,0:T(8,128)(2,1)S(1)}, u32[]{:S(2)}, u32[]{:S(2)}) collective-permute-start(bf16[1,2,4,3,64,128]{5,4,3,2,1,0:T(8,128)(2,1)S(1)} %maximum_bitcast_fusion.1), channel_id=1, source_target_pairs={{0,28},{4,32},{8,36},{12,40},{16,44},{20,48},{24,52},{28,56},{32,6... | collective-permute-start | bytes 1179656 | tf_op jit(solution)/shard_map/ppermute | solution.py:15
  17.4 31.4 %collective-permute-start.2 = (bf16[1,2,4,3,64,128]{5,4,3,2,1,0:T(8,128)(2,1)S(1)}, bf16[1,2,4,3,64,128]{5,4,3,2,1,0:T(8,128)(2,1)S(1)}, u32[]{:S(2)}, u32[]{:S(2)}) collective-permute-start(bf16[1,2,4,3,64,128]{5,4,3,2,1,0:T(8,128)(2,1)S(1)} %maximum_bitcast_fusion.1), channel_id=1, source_target_pairs={{0,24},{4,28},{8,32},{12,36},{16,40},{20,44},{24,48},{28,52},{32,5... | collective-permute-start | bytes 1179656 | tf_op jit(solution)/shard_map/ppermute | solution.py:15
  23.0 30.8 %collective-permute-start.3 = (bf16[1,2,4,3,64,128]{5,4,3,2,1,0:T(8,128)(2,1)S(1)}, bf16[1,2,4,3,64,128]{5,4,3,2,1,0:T(8,128)(2,1)S(1)}, u32[]{:S(2)}, u32[]{:S(2)}) collective-permute-start(bf16[1,2,4,3,64,128]{5,4,3,2,1,0:T(8,128)(2,1)S(1)} %maximum_bitcast_fusion.1), channel_id=1, source_target_pairs={{0,20},{4,24},{8,28},{12,32},{16,36},{20,40},{24,44},{28,48},{32,5... | collective-permute-start | bytes 1179656 | tf_op jit(solution)/shard_map/ppermute | solution.py:15
  25.1 30.7 %collective-permute-start.4 = (bf16[1,2,4,3,64,128]{5,4,3,2,1,0:T(8,128)(2,1)S(1)}, bf16[1,2,4,3,64,128]{5,4,3,2,1,0:T(8,128)(2,1)S(1)}, u32[]{:S(2)}, u32[]{:S(2)}) collective-permute-start(bf16[1,2,4,3,64,128]{5,4,3,2,1,0:T(8,128)(2,1)S(1)} %maximum_bitcast_fusion.1), channel_id=1, source_target_pairs={{0,16},{4,20},{8,24},{12,28},{16,32},{20,36},{24,40},{28,44},{32,4... | collective-permute-start | bytes 1179656 | tf_op jit(solution)/shard_map/ppermute | solution.py:15
  30.3 26.8 %collective-permute-start.5 = (bf16[1,2,4,3,64,128]{5,4,3,2,1,0:T(8,128)(2,1)S(1)}, bf16[1,2,4,3,64,128]{5,4,3,2,1,0:T(8,128)(2,1)S(1)}, u32[]{:S(2)}, u32[]{:S(2)}) collective-permute-start(bf16[1,2,4,3,64,128]{5,4,3,2,1,0:T(8,128)(2,1)S(1)} %maximum_bitcast_fusion.1), channel_id=1, source_target_pairs={{0,12},{4,16},{8,20},{12,24},{16,28},{20,32},{24,36},{28,40},{32,4... | collective-permute-start | bytes 1179656 | tf_op jit(solution)/shard_map/ppermute | solution.py:15
  32.9 25.5 %collective-permute-start.6 = (bf16[1,2,4,3,64,128]{5,4,3,2,1,0:T(8,128)(2,1)S(1)}, bf16[1,2,4,3,64,128]{5,4,3,2,1,0:T(8,128)(2,1)S(1)}, u32[]{:S(2)}, u32[]{:S(2)}) collective-permute-start(bf16[1,2,4,3,64,128]{5,4,3,2,1,0:T(8,128)(2,1)S(1)} %maximum_bitcast_fusion.1), channel_id=1, source_target_pairs={{0,8},{4,12},{8,16},{12,20},{16,24},{20,28},{24,32},{28,36},{32,40... | collective-permute-start | bytes 1179656 | tf_op jit(solution)/shard_map/ppermute | solution.py:15
  48.8 11.4 %collective-permute-start.7 = (bf16[1,2,4,3,64,128]{5,4,3,2,1,0:T(8,128)(2,1)S(1)}, bf16[1,2,4,3,64,128]{5,4,3,2,1,0:T(8,128)(2,1)S(1)}, u32[]{:S(2)}, u32[]{:S(2)}) collective-permute-start(bf16[1,2,4,3,64,128]{5,4,3,2,1,0:T(8,128)(2,1)S(1)} %maximum_bitcast_fusion.1), channel_id=1, source_target_pairs={{0,4},{4,8},{8,12},{12,16},{16,20},{20,24},{24,28},{28,32},{32,36}... | collective-permute-start | bytes 1179656 | tf_op jit(solution)/shard_map/ppermute | solution.py:15
  53.8 11.9 %collective-permute-start.8 = (bf16[1,2,4,3,64,128]{5,4,3,2,1,0:T(8,128)(2,1)S(1)}, bf16[1,2,4,3,64,128]{5,4,3,2,1,0:T(8,128)(2,1)S(1)}, u32[]{:S(2)}, u32[]{:S(2)}) collective-permute-start(bf16[1,2,4,3,64,128]{5,4,3,2,1,0:T(8,128)(2,1)S(1)} %maximum_bitcast_fusion.1), channel_id=1, source_target_pairs={{4,0},{8,4},{12,8},{16,12},{20,16},{24,20},{28,24},{32,28},{36,32}... | collective-permute-start | bytes 1179656 | tf_op jit(solution)/shard_map/ppermute | solution.py:15
  55.8 13.0 %collective-permute-start.9 = (bf16[1,2,4,3,64,128]{5,4,3,2,1,0:T(8,128)(2,1)S(1)}, bf16[1,2,4,3,64,128]{5,4,3,2,1,0:T(8,128)(2,1)S(1)}, u32[]{:S(2)}, u32[]{:S(2)}) collective-permute-start(bf16[1,2,4,3,64,128]{5,4,3,2,1,0:T(8,128)(2,1)S(1)} %maximum_bitcast_fusion.1), channel_id=1, source_target_pairs={{8,0},{12,4},{16,8},{20,12},{24,16},{28,20},{32,24},{36,28},{40,32... | collective-permute-start | bytes 1179656 | tf_op jit(solution)/shard_map/ppermute | solution.py:15
  57.2 14.5 %collective-permute-start.10 = (bf16[1,2,4,3,64,128]{5,4,3,2,1,0:T(8,128)(2,1)S(1)}, bf16[1,2,4,3,64,128]{5,4,3,2,1,0:T(8,128)(2,1)S(1)}, u32[]{:S(2)}, u32[]{:S(2)}) collective-permute-start(bf16[1,2,4,3,64,128]{5,4,3,2,1,0:T(8,128)(2,1)S(1)} %maximum_bitcast_fusion.1), channel_id=1, source_target_pairs={{12,0},{16,4},{20,8},{24,12},{28,16},{32,20},{36,24},{40,28},{44,3... | collective-permute-start | bytes 1179656 | tf_op jit(solution)/shard_map/ppermute | solution.py:15
  58.5 19.3 %collective-permute-start.11 = (bf16[1,2,4,3,64,128]{5,4,3,2,1,0:T(8,128)(2,1)S(1)}, bf16[1,2,4,3,64,128]{5,4,3,2,1,0:T(8,128)(2,1)S(1)}, u32[]{:S(2)}, u32[]{:S(2)}) collective-permute-start(bf16[1,2,4,3,64,128]{5,4,3,2,1,0:T(8,128)(2,1)S(1)} %maximum_bitcast_fusion.1), channel_id=1, source_target_pairs={{16,0},{20,4},{24,8},{28,12},{32,16},{36,20},{40,24},{44,28},{48,3... | collective-permute-start | bytes 1179656 | tf_op jit(solution)/shard_map/ppermute | solution.py:15
  60.2 28.4 %collective-permute-start.12 = (bf16[1,2,4,3,64,128]{5,4,3,2,1,0:T(8,128)(2,1)S(1)}, bf16[1,2,4,3,64,128]{5,4,3,2,1,0:T(8,128)(2,1)S(1)}, u32[]{:S(2)}, u32[]{:S(2)}) collective-permute-start(bf16[1,2,4,3,64,128]{5,4,3,2,1,0:T(8,128)(2,1)S(1)} %maximum_bitcast_fusion.1), channel_id=1, source_target_pairs={{20,0},{24,4},{28,8},{32,12},{36,16},{40,20},{44,24},{48,28},{52,3... | collective-permute-start | bytes 1179656 | tf_op jit(solution)/shard_map/ppermute | solution.py:15
  65.7 31.3 %collective-permute-start.13 = (bf16[1,2,4,3,64,128]{5,4,3,2,1,0:T(8,128)(2,1)S(1)}, bf16[1,2,4,3,64,128]{5,4,3,2,1,0:T(8,128)(2,1)S(1)}, u32[]{:S(2)}, u32[]{:S(2)}) collective-permute-start(bf16[1,2,4,3,64,128]{5,4,3,2,1,0:T(8,128)(2,1)S(1)} %maximum_bitcast_fusion.1), channel_id=1, source_target_pairs={{24,0},{28,4},{32,8},{36,12},{40,16},{44,20},{48,24},{52,28},{56,3... | collective-permute-start | bytes 1179656 | tf_op jit(solution)/shard_map/ppermute | solution.py:15
  68.8 50.5 %collective-permute-start.14 = (bf16[1,2,4,3,64,128]{5,4,3,2,1,0:T(8,128)(2,1)S(1)}, bf16[1,2,4,3,64,128]{5,4,3,2,1,0:T(8,128)(2,1)S(1)}, u32[]{:S(2)}, u32[]{:S(2)}) collective-permute-start(bf16[1,2,4,3,64,128]{5,4,3,2,1,0:T(8,128)(2,1)S(1)} %maximum_bitcast_fusion.1), channel_id=1, source_target_pairs={{28,0},{32,4},{36,8},{40,12},{44,16},{48,20},{52,24},{56,28},{60,3... | collective-permute-start | bytes 1179656 | tf_op jit(solution)/shard_map/ppermute | solution.py:15
  71.6 49.3 %collective-permute-start.15 = (bf16[1,2,4,3,64,128]{5,4,3,2,1,0:T(8,128)(2,1)S(1)}, bf16[1,2,4,3,64,128]{5,4,3,2,1,0:T(8,128)(2,1)S(1)}, u32[]{:S(2)}, u32[]{:S(2)}) collective-permute-start(bf16[1,2,4,3,64,128]{5,4,3,2,1,0:T(8,128)(2,1)S(1)} %maximum_bitcast_fusion.1), channel_id=1, source_target_pairs={{32,0},{36,4},{40,8},{44,12},{48,16},{52,20},{56,24},{60,28},{64,3... | collective-permute-start | bytes 1179656 | tf_op jit(solution)/shard_map/ppermute | solution.py:15
  145.3 20.7 %copy-start.73 = (s32[2]{0:T(128)}, s32[2]{0:T(128)S(1)}, u32[]{:S(2)}) copy-start(s32[2]{0:T(128)S(1)} %get-tuple-element.1728) | copy-start | bytes 28 | tf_op jit(solution)/shard_map/while
  166.0 11.4 %copy-start.12 = (bf16[64,3,128]{2,1,0:T(4,128)(2,1)}, bf16[64,3,128]{2,1,0:T(4,128)(2,1)S(1)}, u32[]{:S(2)}) copy-start(bf16[64,3,128]{2,1,0:T(4,128)(2,1)S(1)} %get-tuple-element.1514) | copy-start | bytes 147460 | tf_op jit(solution)/shard_map/while
  166.0 11.4 %copy-start.13 = (bf16[64,3,128]{2,1,0:T(4,128)(2,1)}, bf16[64,3,128]{2,1,0:T(4,128)(2,1)S(1)}, u32[]{:S(2)}) copy-start(bf16[64,3,128]{2,1,0:T(4,128)(2,1)S(1)} %get-tuple-element.1515) | copy-start | bytes 147460 | tf_op jit(solution)/shard_map/while
  174.1 19.6 %copy-start.3 = (bf16[64,64,128]{2,1,0:T(8,128)(2,1)}, bf16[64,64,128]{2,1,0:T(8,128)(2,1)S(1)}, u32[]{:S(2)}) copy-start(bf16[64,64,128]{2,1,0:T(8,128)(2,1)S(1)} %fusion.229) | copy-start | bytes 3145732 | tf_op jit(solution)/shard_map/while
  203.5 20.7 %copy-start.2 = (bf16[4096,512]{1,0:T(8,128)(2,1)}, bf16[4096,512]{1,0:T(8,128)(2,1)S(1)}, u32[]{:S(2)}) copy-start(bf16[4096,512]{1,0:T(8,128)(2,1)S(1)} %get-tuple-element.1641) | copy-start | bytes 12582916 | tf_op jit(solution)/shard_map/while
  214.1 9.7 %copy-start.10 = (bf16[2,64,64,128]{3,2,1,0:T(8,128)(2,1)S(1)}, bf16[2,64,64,128]{3,2,1,0:T(8,128)(2,1)}, u32[]{:S(2)}) copy-start(bf16[2,64,64,128]{3,2,1,0:T(8,128)(2,1)} %get-tuple-element.1691) | copy-start | bytes 6291460 | tf_op jit(solution)/shard_map/while
  237.2 8.8 %copy-start.27 = (f32[128]{0:T(128)S(1)}, f32[128]{0:T(128)}, u32[]{:S(2)}) copy-start(f32[128]{0:T(128)} %get-tuple-element.1619) | copy-start | bytes 1540 | tf_op jit(solution)/shard_map/while
  237.2 8.8 %copy-start.28 = (f32[128]{0:T(128)S(1)}, f32[128]{0:T(128)}, u32[]{:S(2)}) copy-start(f32[128]{0:T(128)} %get-tuple-element.1618) | copy-start | bytes 1540 | tf_op jit(solution)/shard_map/while
  237.2 8.8 %copy-start.29 = (f32[128]{0:T(128)S(1)}, f32[128]{0:T(128)}, u32[]{:S(2)}) copy-start(f32[128]{0:T(128)} %get-tuple-element.1617) | copy-start | bytes 1540 | tf_op jit(solution)/shard_map/while
  237.3 8.7 %copy-start.30 = (f32[128]{0:T(128)S(1)}, f32[128]{0:T(128)}, u32[]{:S(2)}) copy-start(f32[128]{0:T(128)} %get-tuple-element.1616) | copy-start | bytes 1540 | tf_op jit(solution)/shard_map/while
  247.5 7.3 copy-start.22
  247.5 7.3 copy-start.8
  259.4 20.7 %copy-start.73 = (s32[2]{0:T(128)}, s32[2]{0:T(128)S(1)}, u32[]{:S(2)}) copy-start(s32[2]{0:T(128)S(1)} %get-tuple-element.1728) | copy-start | bytes 28 | tf_op jit(solution)/shard_map/while
  280.0 11.4 %copy-start.12 = (bf16[64,3,128]{2,1,0:T(4,128)(2,1)}, bf16[64,3,128]{2,1,0:T(4,128)(2,1)S(1)}, u32[]{:S(2)}) copy-start(bf16[64,3,128]{2,1,0:T(4,128)(2,1)S(1)} %get-tuple-element.1514) | copy-start | bytes 147460 | tf_op jit(solution)/shard_map/while
  280.0 11.4 %copy-start.13 = (bf16[64,3,128]{2,1,0:T(4,128)(2,1)}, bf16[64,3,128]{2,1,0:T(4,128)(2,1)S(1)}, u32[]{:S(2)}) copy-start(bf16[64,3,128]{2,1,0:T(4,128)(2,1)S(1)} %get-tuple-element.1515) | copy-start | bytes 147460 | tf_op jit(solution)/shard_map/while
  288.1 19.6 %copy-start.3 = (bf16[64,64,128]{2,1,0:T(8,128)(2,1)}, bf16[64,64,128]{2,1,0:T(8,128)(2,1)S(1)}, u32[]{:S(2)}) copy-start(bf16[64,64,128]{2,1,0:T(8,128)(2,1)S(1)} %fusion.229) | copy-start | bytes 3145732 | tf_op jit(solution)/shard_map/while
  317.6 20.7 %copy-start.2 = (bf16[4096,512]{1,0:T(8,128)(2,1)}, bf16[4096,512]{1,0:T(8,128)(2,1)S(1)}, u32[]{:S(2)}) copy-start(bf16[4096,512]{1,0:T(8,128)(2,1)S(1)} %get-tuple-element.1641) | copy-start | bytes 12582916 | tf_op jit(solution)/shard_map/while
  328.1 9.7 %copy-start.10 = (bf16[2,64,64,128]{3,2,1,0:T(8,128)(2,1)S(1)}, bf16[2,64,64,128]{3,2,1,0:T(8,128)(2,1)}, u32[]{:S(2)}) copy-start(bf16[2,64,64,128]{3,2,1,0:T(8,128)(2,1)} %get-tuple-element.1691) | copy-start | bytes 6291460 | tf_op jit(solution)/shard_map/while
  351.3 8.8 %copy-start.27 = (f32[128]{0:T(128)S(1)}, f32[128]{0:T(128)}, u32[]{:S(2)}) copy-start(f32[128]{0:T(128)} %get-tuple-element.1619) | copy-start | bytes 1540 | tf_op jit(solution)/shard_map/while
  351.3 8.8 %copy-start.28 = (f32[128]{0:T(128)S(1)}, f32[128]{0:T(128)}, u32[]{:S(2)}) copy-start(f32[128]{0:T(128)} %get-tuple-element.1618) | copy-start | bytes 1540 | tf_op jit(solution)/shard_map/while
  351.3 8.8 %copy-start.29 = (f32[128]{0:T(128)S(1)}, f32[128]{0:T(128)}, u32[]{:S(2)}) copy-start(f32[128]{0:T(128)} %get-tuple-element.1617) | copy-start | bytes 1540 | tf_op jit(solution)/shard_map/while
  351.3 8.7 %copy-start.30 = (f32[128]{0:T(128)S(1)}, f32[128]{0:T(128)}, u32[]{:S(2)}) copy-start(f32[128]{0:T(128)} %get-tuple-element.1616) | copy-start | bytes 1540 | tf_op jit(solution)/shard_map/while
  361.5 7.3 copy-start.22
  361.5 7.3 copy-start.8
  373.6 22.7 %copy-start.21 = (f32[7,7,128]{2,1,0:T(8,128)S(1)}, f32[7,7,128]{2,1,0:T(8,128)}, u32[]{:S(2)}) copy-start(f32[7,7,128]{2,1,0:T(8,128)} %get-tuple-element.2208) | copy-start | bytes 75268
  373.6 22.7 %copy-start.24 = (f32[512]{0:T(512)S(1)}, f32[512]{0:T(512)}, u32[]{:S(2)}) copy-start(f32[512]{0:T(512)} %get-tuple-element.2213) | copy-start | bytes 6148
  373.6 22.7 %copy-start.48 = (f32[128]{0:T(128)S(1)}, f32[128]{0:T(128)}, u32[]{:S(2)}) copy-start(f32[128]{0:T(128)} %get-tuple-element.2216) | copy-start | bytes 1540
  373.7 22.7 %copy-start.51 = (f32[128]{0:T(128)S(1)}, f32[128]{0:T(128)}, u32[]{:S(2)}) copy-start(f32[128]{0:T(128)} %get-tuple-element.2209) | copy-start | bytes 1540
  373.7 22.7 %copy-start.54 = (f32[128]{0:T(128)S(1)}, f32[128]{0:T(128)}, u32[]{:S(2)}) copy-start(f32[128]{0:T(128)} %get-tuple-element.2210) | copy-start | bytes 1540
  373.7 22.7 %copy-start.57 = (f32[128]{0:T(128)S(1)}, f32[128]{0:T(128)}, u32[]{:S(2)}) copy-start(f32[128]{0:T(128)} %get-tuple-element.2211) | copy-start | bytes 1540
  373.7 22.7 %copy-start.60 = (f32[128]{0:T(128)S(1)}, f32[128]{0:T(128)}, u32[]{:S(2)}) copy-start(f32[128]{0:T(128)} %get-tuple-element.2215) | copy-start | bytes 1540
  376.5 252.5 %collective-permute-start.23 = (bf16[1,2,4,3,64,128]{5,3,4,1,0,2:T(4,128)(2,1)S(1)}, bf16[1,2,4,3,64,128]{5,3,4,1,0,2:T(4,128)(2,1)S(1)}, u32[]{:S(2)}, u32[]{:S(2)}) collective-permute-start(bf16[1,2,4,3,64,128]{5,3,4,1,0,2:T(4,128)(2,1)S(1)} %maximum_bitcast_fusion), channel_id=1, source_target_pairs={{0,4},{4,8},{8,12},{12,16},{16,20},{20,24},{24,28},{28,32},{32,36}... | collective-permute-start | bytes 1179656 | tf_op jit(solution)/shard_map/ppermute | solution.py:15
  383.0 249.6 %collective-permute-start.24 = (bf16[1,2,4,3,64,128]{5,3,4,1,0,2:T(4,128)(2,1)S(1)}, bf16[1,2,4,3,64,128]{5,3,4,1,0,2:T(4,128)(2,1)S(1)}, u32[]{:S(2)}, u32[]{:S(2)}) collective-permute-start(bf16[1,2,4,3,64,128]{5,3,4,1,0,2:T(4,128)(2,1)S(1)} %maximum_bitcast_fusion), channel_id=1, source_target_pairs={{4,0},{8,4},{12,8},{16,12},{20,16},{24,20},{28,24},{32,28},{36,32}... | collective-permute-start | bytes 1179656 | tf_op jit(solution)/shard_map/ppermute | solution.py:15
  385.0 251.9 %collective-permute-start.16 = (bf16[1,2,4,3,64,128]{5,3,4,1,0,2:T(4,128)(2,1)S(1)}, bf16[1,2,4,3,64,128]{5,3,4,1,0,2:T(4,128)(2,1)}, u32[]{:S(2)}, u32[]{:S(2)}) collective-permute-start(bf16[1,2,4,3,64,128]{5,3,4,1,0,2:T(4,128)(2,1)S(1)} %maximum_bitcast_fusion), channel_id=1, source_target_pairs={{0,32},{4,36},{8,40},{12,44},{16,48},{20,52},{24,56},{28,60},{32,6... | collective-permute-start | bytes 1179656 | tf_op jit(solution)/shard_map/ppermute | solution.py:15
  389.0 254.9 %collective-permute-start.17 = (bf16[1,2,4,3,64,128]{5,3,4,1,0,2:T(4,128)(2,1)S(1)}, bf16[1,2,4,3,64,128]{5,3,4,1,0,2:T(4,128)(2,1)}, u32[]{:S(2)}, u32[]{:S(2)}) collective-permute-start(bf16[1,2,4,3,64,128]{5,3,4,1,0,2:T(4,128)(2,1)S(1)} %maximum_bitcast_fusion), channel_id=1, source_target_pairs={{0,28},{4,32},{8,36},{12,40},{16,44},{20,48},{24,52},{28,56},{32,6... | collective-permute-start | bytes 1179656 | tf_op jit(solution)/shard_map/ppermute | solution.py:15
  395.0 252.5 %collective-permute-start.18 = (bf16[1,2,4,3,64,128]{5,3,4,1,0,2:T(4,128)(2,1)S(1)}, bf16[1,2,4,3,64,128]{5,3,4,1,0,2:T(4,128)(2,1)S(1)}, u32[]{:S(2)}, u32[]{:S(2)}) collective-permute-start(bf16[1,2,4,3,64,128]{5,3,4,1,0,2:T(4,128)(2,1)S(1)} %maximum_bitcast_fusion), channel_id=1, source_target_pairs={{0,24},{4,28},{8,32},{12,36},{16,40},{20,44},{24,48},{28,52},{32,5... | collective-permute-start | bytes 1179656 | tf_op jit(solution)/shard_map/ppermute | solution.py:15
  629.0 54.6 %collective-permute-start.19 = (bf16[1,2,4,3,64,128]{5,3,4,1,0,2:T(4,128)(2,1)S(1)}, bf16[1,2,4,3,64,128]{5,3,4,1,0,2:T(4,128)(2,1)S(1)}, u32[]{:S(2)}, u32[]{:S(2)}) collective-permute-start(bf16[1,2,4,3,64,128]{5,3,4,1,0,2:T(4,128)(2,1)S(1)} %maximum_bitcast_fusion), channel_id=1, source_target_pairs={{0,20},{4,24},{8,28},{12,32},{16,36},{20,40},{24,44},{28,48},{32,5... | collective-permute-start | bytes 1179656 | tf_op jit(solution)/shard_map/ppermute | solution.py:15
  632.6 52.4 %collective-permute-start.20 = (bf16[1,2,4,3,64,128]{5,3,4,1,0,2:T(4,128)(2,1)S(1)}, bf16[1,2,4,3,64,128]{5,3,4,1,0,2:T(4,128)(2,1)S(1)}, u32[]{:S(2)}, u32[]{:S(2)}) collective-permute-start(bf16[1,2,4,3,64,128]{5,3,4,1,0,2:T(4,128)(2,1)S(1)} %maximum_bitcast_fusion), channel_id=1, source_target_pairs={{0,16},{4,20},{8,24},{12,28},{16,32},{20,36},{24,40},{28,44},{32,4... | collective-permute-start | bytes 1179656 | tf_op jit(solution)/shard_map/ppermute | solution.py:15
  636.9 49.6 %collective-permute-start.21 = (bf16[1,2,4,3,64,128]{5,3,4,1,0,2:T(4,128)(2,1)S(1)}, bf16[1,2,4,3,64,128]{5,3,4,1,0,2:T(4,128)(2,1)S(1)}, u32[]{:S(2)}, u32[]{:S(2)}) collective-permute-start(bf16[1,2,4,3,64,128]{5,3,4,1,0,2:T(4,128)(2,1)S(1)} %maximum_bitcast_fusion), channel_id=1, source_target_pairs={{0,12},{4,16},{8,20},{12,24},{16,28},{20,32},{24,36},{28,40},{32,4... | collective-permute-start | bytes 1179656 | tf_op jit(solution)/shard_map/ppermute | solution.py:15
  644.0 43.9 %collective-permute-start.22 = (bf16[1,2,4,3,64,128]{5,3,4,1,0,2:T(4,128)(2,1)S(1)}, bf16[1,2,4,3,64,128]{5,3,4,1,0,2:T(4,128)(2,1)S(1)}, u32[]{:S(2)}, u32[]{:S(2)}) collective-permute-start(bf16[1,2,4,3,64,128]{5,3,4,1,0,2:T(4,128)(2,1)S(1)} %maximum_bitcast_fusion), channel_id=1, source_target_pairs={{0,8},{4,12},{8,16},{12,20},{16,24},{20,28},{24,32},{28,36},{32,40... | collective-permute-start | bytes 1179656 | tf_op jit(solution)/shard_map/ppermute | solution.py:15
  647.5 44.0 %collective-permute-start.25 = (bf16[1,2,4,3,64,128]{5,3,4,1,0,2:T(4,128)(2,1)S(1)}, bf16[1,2,4,3,64,128]{5,3,4,1,0,2:T(4,128)(2,1)S(1)}, u32[]{:S(2)}, u32[]{:S(2)}) collective-permute-start(bf16[1,2,4,3,64,128]{5,3,4,1,0,2:T(4,128)(2,1)S(1)} %maximum_bitcast_fusion), channel_id=1, source_target_pairs={{8,0},{12,4},{16,8},{20,12},{24,16},{28,20},{32,24},{36,28},{40,32... | collective-permute-start | bytes 1179656 | tf_op jit(solution)/shard_map/ppermute | solution.py:15
  683.6 28.3 %collective-permute-start.26 = (bf16[1,2,4,3,64,128]{5,3,4,1,0,2:T(4,128)(2,1)S(1)}, bf16[1,2,4,3,64,128]{5,3,4,1,0,2:T(4,128)(2,1)S(1)}, u32[]{:S(2)}, u32[]{:S(2)}) collective-permute-start(bf16[1,2,4,3,64,128]{5,3,4,1,0,2:T(4,128)(2,1)S(1)} %maximum_bitcast_fusion), channel_id=1, source_target_pairs={{12,0},{16,4},{20,8},{24,12},{28,16},{32,20},{36,24},{40,28},{44,3... | collective-permute-start | bytes 1179656 | tf_op jit(solution)/shard_map/ppermute | solution.py:15
  685.1 30.6 %collective-permute-start.27 = (bf16[1,2,4,3,64,128]{5,3,4,1,0,2:T(4,128)(2,1)S(1)}, bf16[1,2,4,3,64,128]{5,3,4,1,0,2:T(4,128)(2,1)S(1)}, u32[]{:S(2)}, u32[]{:S(2)}) collective-permute-start(bf16[1,2,4,3,64,128]{5,3,4,1,0,2:T(4,128)(2,1)S(1)} %maximum_bitcast_fusion), channel_id=1, source_target_pairs={{16,0},{20,4},{24,8},{28,12},{32,16},{36,20},{40,24},{44,28},{48,3... | collective-permute-start | bytes 1179656 | tf_op jit(solution)/shard_map/ppermute | solution.py:15
  686.5 29.3 %collective-permute-start.28 = (bf16[1,2,4,3,64,128]{5,3,4,1,0,2:T(4,128)(2,1)S(1)}, bf16[1,2,4,3,64,128]{5,3,4,1,0,2:T(4,128)(2,1)S(1)}, u32[]{:S(2)}, u32[]{:S(2)}) collective-permute-start(bf16[1,2,4,3,64,128]{5,3,4,1,0,2:T(4,128)(2,1)S(1)} %maximum_bitcast_fusion), channel_id=1, source_target_pairs={{20,0},{24,4},{28,8},{32,12},{36,16},{40,20},{44,24},{48,28},{52,3... | collective-permute-start | bytes 1179656 | tf_op jit(solution)/shard_map/ppermute | solution.py:15
  687.9 28.0 %collective-permute-start.29 = (bf16[1,2,4,3,64,128]{5,3,4,1,0,2:T(4,128)(2,1)S(1)}, bf16[1,2,4,3,64,128]{5,3,4,1,0,2:T(4,128)(2,1)S(1)}, u32[]{:S(2)}, u32[]{:S(2)}) collective-permute-start(bf16[1,2,4,3,64,128]{5,3,4,1,0,2:T(4,128)(2,1)S(1)} %maximum_bitcast_fusion), channel_id=1, source_target_pairs={{24,0},{28,4},{32,8},{36,12},{40,16},{44,20},{48,24},{52,28},{56,3... | collective-permute-start | bytes 1179656 | tf_op jit(solution)/shard_map/ppermute | solution.py:15
  691.6 47.0 %collective-permute-start.30 = (bf16[1,2,4,3,64,128]{5,3,4,1,0,2:T(4,128)(2,1)S(1)}, bf16[1,2,4,3,64,128]{5,3,4,1,0,2:T(4,128)(2,1)S(1)}, u32[]{:S(2)}, u32[]{:S(2)}) collective-permute-start(bf16[1,2,4,3,64,128]{5,3,4,1,0,2:T(4,128)(2,1)S(1)} %maximum_bitcast_fusion), channel_id=1, source_target_pairs={{28,0},{32,4},{36,8},{40,12},{44,16},{48,20},{52,24},{56,28},{60,3... | collective-permute-start | bytes 1179656 | tf_op jit(solution)/shard_map/ppermute | solution.py:15
  711.9 41.4 %collective-permute-start.31 = (bf16[1,2,4,3,64,128]{5,3,4,1,0,2:T(4,128)(2,1)S(1)}, bf16[1,2,4,3,64,128]{5,3,4,1,0,2:T(4,128)(2,1)S(1)}, u32[]{:S(2)}, u32[]{:S(2)}) collective-permute-start(bf16[1,2,4,3,64,128]{5,3,4,1,0,2:T(4,128)(2,1)S(1)} %maximum_bitcast_fusion), channel_id=1, source_target_pairs={{32,0},{36,4},{40,8},{44,12},{48,16},{52,20},{56,24},{60,28},{64,3... | collective-permute-start | bytes 1179656 | tf_op jit(solution)/shard_map/ppermute | solution.py:15
  (99 other events, 388.3 us)
Sparse Core Ops, SparseCore 0:
  481.8 143.7 all-reduce.3
where the time goes:
time: 875 us; the launch traced here: 866 us
  waiting for transfers between devices  310 us (35%)
  other arithmetic  160 us (18%)
  loops' own time  110 us (13%)
  starting transfers between devices  82.6 us (9%)
  blocking collectives  82.6 us (9%)
  local copies, waits for them, and re-layouts  56.4 us (6%)
  matrix products  48.5 us (6%)
  between operations  15.3 us (2%)
    ppermute x32, waiting for transfers between devices, passed_along(): return lax.ppermute(value, axis, pairs)  167 us
    psum x1, waiting for transfers between devices, local(): lax.psum((grad_sums[0], grad_sums[1], grad_sums[2], grad_sums[3], grad_su...  143 us
    psum x1, blocking collectives, local(): lax.psum((grad_sums[0], grad_sums[1], grad_sums[2], grad_sums[3], grad_su...  82.6 us
    ppermute x32, starting transfers between devices, passed_along(): return lax.ppermute(value, axis, pairs)  82.5 us
    another operation x1, loops' own time, local(): lax.scan(first_step, grad_sums, jnp.arange(slot_count))  63 us
    another operation x1, loops' own time, local(): outputs = [lax.map(second_step, jnp.arange(slot_count))]  47.2 us
    reduce_sum x6, other arithmetic, kernel_terms(): line_terms.append(jnp.sum(grad_values * window, axis=(0, 1)))  47.1 us
    dynamic_update_slice x2, other arithmetic, local(): lax.scan(first_step, grad_sums, jnp.arange(slot_count))  33.4 us
  transfers between devices with their start and end apart: 33, of which 18 were waited for; matrix products, arithmetic and copies ran while one was open for 1% of the time, Pallas kernels for 0%

commit v1 on v0

--- a/solution.py
+++ b/solution.py
@@ -255,18 +255,21 @@
 
     outputs = [lax.map(second_step, jnp.arange(slot_count))]
     summed = lax.psum(
-        (
-            grad_sums[0],
-            grad_sums[1],
-            grad_sums[2],
-            grad_sums[3],
-            grad_sums[4],
-            grad_sums[5],
-            grad_sums[6],
-            grad_sums[7],
-            grad_sums[8],
+        lax.psum(
+            (
+                grad_sums[0],
+                grad_sums[1],
+                grad_sums[2],
+                grad_sums[3],
+                grad_sums[4],
+                grad_sums[5],
+                grad_sums[6],
+                grad_sums[7],
+                grad_sums[8],
+            ),
+            "dp",
         ),
-        ("tile", "dp"),
+        "tile",
     )
     grad_scale = 1.0 / math.sqrt(
         samples * lax.axis_size("dp") * slot_count * tile_count * extent * extent

time: 875 us -> 782 us (0.89)
  waiting for transfers between devices: 310 us -> 178 us
  blocking collectives: 82.6 us -> 135 us
  starting transfers between devices: 82.6 us -> 72.2 us
    psum x1, waiting for transfers between devices: 143 us -> 0.02 us  [local(): lax.psum((grad_sums[0], grad_sums[1], grad_sums[2], grad_sums[3], grad_su...]
    psum x0 -> x1, blocking collectives: none -> 120 us  [local(): lax.psum(lax.psum((grad_sums[0], grad_sums[1], grad_sums[2], grad_sums[3]...]
    psum x1, blocking collectives: 82.6 us -> 14.2 us  [local(): lax.psum((grad_sums[0], grad_sums[1], grad_sums[2], grad_sums[3], grad_su...]
    ppermute x32, starting transfers between devices: 82.5 us -> 72.1 us  [passed_along(): return lax.ppermute(value, axis, pairs)]
  transfers between devices with their start and end apart: 33 -> 34, of which waited for: 18 -> 19; matrix products, arithmetic and copies ran while one was open for 1% -> 8% of each run, Pallas kernels for 0% -> 0%
where the time goes in v1:
time: 782 us; the launch traced here: 773 us
  waiting for transfers between devices  178 us (23%)
  other arithmetic  160 us (20%)
  blocking collectives  135 us (17%)
  loops' own time  110 us (14%)
  starting transfers between devices  72.2 us (9%)
  local copies, waits for them, and re-layouts  54.1 us (7%)
  matrix products  48.5 us (6%)
  between operations  15.3 us (2%)
    ppermute x32, waiting for transfers between devices, passed_along(): return lax.ppermute(value, axis, pairs)  175 us
    psum x1, blocking collectives, local(): lax.psum(lax.psum((grad_sums[0], grad_sums[1], grad_sums[2], grad_sums[3]...  120 us
    ppermute x32, starting transfers between devices, passed_along(): return lax.ppermute(value, axis, pairs)  72.1 us
    another operation x1, loops' own time, local(): lax.scan(first_step, grad_sums, jnp.arange(slot_count))  63 us
    reduce_sum x6, other arithmetic, kernel_terms(): line_terms.append(jnp.sum(grad_values * window, axis=(0, 1)))  47.1 us
    another operation x1, loops' own time, local(): outputs = [lax.map(second_step, jnp.arange(slot_count))]  46.6 us
    dynamic_update_slice x2, other arithmetic, local(): lax.scan(first_step, grad_sums, jnp.arange(slot_count))  33.4 us
    reduce_sum x2, other arithmetic, layer_rows(): mean_value = jnp.mean(conv_rows, -1, keepdims=True)  32.5 us
  transfers between devices with their start and end apart: 34, of which 19 were waited for; matrix products, arithmetic and copies ran while one was open for 8% of the time, Pallas kernels for 0%

profile of v1, /device:TPU:1, one launch (start us, length us, event | category | flops | bytes accessed | tf_op | source)
XLA Modules:
  0.0 772.7 jit_solution(12727644815052351091)
XLA Ops:
  9.4 4.0 collective-permute-start
  13.4 4.0 collective-permute-start.1
  17.4 5.7 collective-permute-start.2
  23.0 2.0 collective-permute-start.3
  25.1 5.1 collective-permute-start.4
  30.3 2.6 collective-permute-start.5
  32.9 2.7 collective-permute-start.6
  35.7 13.1 %collective-permute-done.2 = bf16[1,2,4,3,64,128]{5,4,3,2,1,0:T(8,128)(2,1)S(1)} collective-permute-done((bf16[1,2,4,3,64,128]{5,4,3,2,1,0:T(8,128)(2,1)S(1)}, bf16[1,2,4,3,64,128]{5,4,3,2,1,0:T(8,128)(2,1)S(1)}, u32[]{:S(2)}, u32[]{:S(2)}) %collective-permute-start.2) | collective-permute-done | bytes 393248 | tf_op jit(solution)/shard_map/ppermute | solution.py:15
  48.8 1.9 collective-permute-start.7
  50.7 3.1 collective-permute-done.3
  53.8 1.9 collective-permute-start.8
  61.6 4.2 collective-permute-done.8
  73.0 4.9 collective-permute-done.11
  77.9 10.7 %collective-permute-done.12 = bf16[1,2,4,3,64,128]{5,4,3,2,1,0:T(8,128)(2,1)S(1)} collective-permute-done((bf16[1,2,4,3,64,128]{5,4,3,2,1,0:T(8,128)(2,1)S(1)}, bf16[1,2,4,3,64,128]{5,4,3,2,1,0:T(8,128)(2,1)S(1)}, u32[]{:S(2)}, u32[]{:S(2)}) %collective-permute-start.12) | collective-permute-done | bytes 393248 | tf_op jit(solution)/shard_map/ppermute | solution.py:15
  88.6 8.4 %collective-permute-done.13 = bf16[1,2,4,3,64,128]{5,4,3,2,1,0:T(8,128)(2,1)S(1)} collective-permute-done((bf16[1,2,4,3,64,128]{5,4,3,2,1,0:T(8,128)(2,1)S(1)}, bf16[1,2,4,3,64,128]{5,4,3,2,1,0:T(8,128)(2,1)S(1)}, u32[]{:S(2)}, u32[]{:S(2)}) %collective-permute-start.13) | collective-permute-done | bytes 393248 | tf_op jit(solution)/shard_map/ppermute | solution.py:15
  97.0 22.3 %collective-permute-done.14 = bf16[1,2,4,3,64,128]{5,4,3,2,1,0:T(8,128)(2,1)S(1)} collective-permute-done((bf16[1,2,4,3,64,128]{5,4,3,2,1,0:T(8,128)(2,1)S(1)}, bf16[1,2,4,3,64,128]{5,4,3,2,1,0:T(8,128)(2,1)S(1)}, u32[]{:S(2)}, u32[]{:S(2)}) %collective-permute-start.14) | collective-permute-done | bytes 393248 | tf_op jit(solution)/shard_map/ppermute | solution.py:15
  121.0 6.8 copy.25
  129.0 1.9 broadcast.179.clone
  130.9 242.7 %while.43 = (s32[]{:T(128)}, f32[7,7,128]{2,1,0:T(8,128)}, f32[128]{0:T(128)}, f32[128]{0:T(128)}, f32[128]{0:T(128)}, /*index=5*/f32[128,512]{1,0:T(8,128)}, f3...) while((s32[]{:T(128)}, f32[7,7,128]{2,1,0:T(8,128)}, ...), condition=%wide.region_60.61_spmd.clone, body=%wide.region_0.60_spmd.clone.sunk | while | flops 3501007360 | bytes 273028160 | solution.py:239
  174.1 3.2 maximum_maximum_fusion.7
  177.4 16.3 %fusion.232 = (f32[64,64]{1,0:T(8,128)S(1)}, f32[64,64,128]{2,1,0:T(8,128)S(1)}) fusion(f32[128]{0:T(128)S(1)} %get-tuple-element.1745, f32[128]{0:T(128)S(1)} %get-tuple-element.1536, bf16[67,70,128]{2,1,0:T(8,128)(2,1)S(1)} %get-tuple-element.1535, f32[128]{0:T(128)S(1)} %get-tuple-element.1537, f32[128]{0:T(128)S(1)} %get-tuple-element.1538, ...), kind=kLoop, calls=%fused_computation.494.clone.1 | loop fusion | flops 87027712 | bytes 47326208 | tf_op jit(solution)/shard_map/while/body/eval_jaxpr/reduce_sum | solution.py:103
  196.4 3.7 add_convert_fusion.2
  200.2 3.3 multiply_convert_fusion.5
  203.7 7.3 convert_reduce_fusion.6
  211.0 3.0 multiply_reduce_fusion.7
  214.1 9.7 %fusion.234 = (f32[128]{0:T(128)}, f32[128]{0:T(128)}, f32[128]{0:T(128)}, f32[128]{0:T(128)}, f32[128]{0:T(128)}, /*index=5*/f32[128]{0:T(128)}, f32[128]{0:T(1...) fusion(bf16[67,70,128]{2,1,0:T(8,128)(2,1)S(1)} %get-tuple-elem, ...), kind=kLoop, calls=%fused_computation.301.clone.1 | loop fusion | flops 33027840 | bytes 24192512 | tf_op jit(solution)/shard_map/while/body/eval_jaxpr/reduce_sum | solution.py:79
  224.4 2.4 fusion.241
  228.7 4.0 fusion.239
  237.3 8.7 %fusion.235 = (f32[128]{0:T(128)}, f32[128]{0:T(128)}, f32[128]{0:T(128)}, f32[128]{0:T(128)}, f32[128]{0:T(128)}, /*index=5*/f32[128]{0:T(128)}, f32[128]{0:T(1...) fusion(bf16[67,70,128]{2,1,0:T(8,128)(2,1)S(1)} %get-tuple-element.1535, ...), kind=kLoop, calls=%fused_computation.283.clone.1 | loop fusion | flops 28834304 | bytes 8493056 | tf_op jit(solution)/shard_map/while/body/eval_jaxpr/reduce_sum | solution.py:79
  247.5 5.2 fusion.236
  252.9 1.8 convert_reduce_fusion.8
  254.9 4.3 fusion.240
  288.1 3.2 maximum_maximum_fusion.7
  291.4 16.3 %fusion.232 = (f32[64,64]{1,0:T(8,128)S(1)}, f32[64,64,128]{2,1,0:T(8,128)S(1)}) fusion(f32[128]{0:T(128)S(1)} %get-tuple-element.1745, f32[128]{0:T(128)S(1)} %get-tuple-element.1536, bf16[67,70,128]{2,1,0:T(8,128)(2,1)S(1)} %get-tuple-element.1535, f32[128]{0:T(128)S(1)} %get-tuple-element.1537, f32[128]{0:T(128)S(1)} %get-tuple-element.1538, ...), kind=kLoop, calls=%fused_computation.494.clone.1 | loop fusion | flops 87027712 | bytes 47326208 | tf_op jit(solution)/shard_map/while/body/eval_jaxpr/reduce_sum | solution.py:103
  310.5 3.7 add_convert_fusion.2
  314.2 3.3 multiply_convert_fusion.5
  317.8 7.3 convert_reduce_fusion.6
  325.1 3.0 multiply_reduce_fusion.7
  328.1 9.7 %fusion.234 = (f32[128]{0:T(128)}, f32[128]{0:T(128)}, f32[128]{0:T(128)}, f32[128]{0:T(128)}, f32[128]{0:T(128)}, /*index=5*/f32[128]{0:T(128)}, f32[128]{0:T(1...) fusion(bf16[67,70,128]{2,1,0:T(8,128)(2,1)S(1)} %get-tuple-elem, ...), kind=kLoop, calls=%fused_computation.301.clone.1 | loop fusion | flops 33027840 | bytes 24192512 | tf_op jit(solution)/shard_map/while/body/eval_jaxpr/reduce_sum | solution.py:79
  338.4 2.4 fusion.241
  342.8 4.0 fusion.239
  351.3 8.7 %fusion.235 = (f32[128]{0:T(128)}, f32[128]{0:T(128)}, f32[128]{0:T(128)}, f32[128]{0:T(128)}, f32[128]{0:T(128)}, /*index=5*/f32[128]{0:T(128)}, f32[128]{0:T(1...) fusion(bf16[67,70,128]{2,1,0:T(8,128)(2,1)S(1)} %get-tuple-element.1535, ...), kind=kLoop, calls=%fused_computation.283.clone.1 | loop fusion | flops 28834304 | bytes 8493056 | tf_op jit(solution)/shard_map/while/body/eval_jaxpr/reduce_sum | solution.py:79
  361.5 5.2 fusion.236
  369.0 4.3 fusion.240
  376.5 6.5 collective-permute-start.23
  383.0 1.9 collective-permute-start.24
  385.0 3.3 collective-permute-start.16
  388.3 6.0 collective-permute-start.17
  395.6 14.2 %all-reduce.2 = (f32[7,7,128]{2,1,0:T(8,128)S(1)}, f32[128]{0:T(128)S(1)}, f32[128]{0:T(128)S(1)}, f32[128]{0:T(128)S(1)}, f32[512]{0:T(512)S(1)}, /*index=5*/f32[128]{0:T(128)S(1)}, f32[128]{0:T(128)S(1)}) all-reduce(f32[7,7,128]{2,1,0:T(8,128)S(1)} %copy-done.21, f32[128]{0:T(128)S(1)} %copy-done.51, ...), channel_id=1, replica_groups=mesh['tile'=32,'dp'=4] {'dp'}, use_global_device_ids=true, to_apply=%region_63.64 | all-reduce | flops 7424 | bytes 59392 | tf_op jit(solution)/shard_map/psum | solution.py:258
  409.9 120.3 %all-reduce = (f32[7,7,128]{2,1,0:T(8,128)S(1)}, f32[128]{0:T(128)S(1)}, f32[128]{0:T(128)S(1)}, f32[128]{0:T(128)S(1)}, f32[512]{0:T(512)S(1)}, /*index=5*/f32[128]{0:T(128)S(1)}, f32[128]{0:T(128)S(1)}) all-reduce(f32[7,7,128]{2,1,0:T(8,128)S(1)} %get-tuple-element.763, ...), channel_id=1, replica_groups=mesh['tile'=32,'dp'=4] {'tile'}, use_global_device_ids=true, to_apply=%region_64.65 | all-reduce | flops 7424 | bytes 59392 | tf_op jit(solution)/shard_map/psum | solution.py:257
  538.4 28.5 %collective-permute-done.19 = bf16[1,2,4,3,64,128]{5,3,4,1,0,2:T(4,128)(2,1)S(1)} collective-permute-done((bf16[1,2,4,3,64,128]{5,3,4,1,0,2:T(4,128)(2,1)S(1)}, bf16[1,2,4,3,64,128]{5,3,4,1,0,2:T(4,128)(2,1)S(1)}, u32[]{:S(2)}, u32[]{:S(2)}) %collective-permute-start.19) | collective-permute-done | bytes 393248 | tf_op jit(solution)/shard_map/ppermute | solution.py:15
  571.2 5.5 collective-permute-done.22
  583.2 7.2 collective-permute-done.26
  591.8 23.7 %collective-permute-done.27 = bf16[1,2,4,3,64,128]{5,3,4,1,0,2:T(4,128)(2,1)S(1)} collective-permute-done((bf16[1,2,4,3,64,128]{5,3,4,1,0,2:T(4,128)(2,1)S(1)}, bf16[1,2,4,3,64,128]{5,3,4,1,0,2:T(4,128)(2,1)S(1)}, u32[]{:S(2)}, u32[]{:S(2)}) %collective-permute-start.27) | collective-permute-done | bytes 393248 | tf_op jit(solution)/shard_map/ppermute | solution.py:15
  617.3 30.6 %collective-permute-done.30 = bf16[1,2,4,3,64,128]{5,3,4,1,0,2:T(4,128)(2,1)S(1)} collective-permute-done((bf16[1,2,4,3,64,128]{5,3,4,1,0,2:T(4,128)(2,1)S(1)}, bf16[1,2,4,3,64,128]{5,3,4,1,0,2:T(4,128)(2,1)S(1)}, u32[]{:S(2)}, u32[]{:S(2)}) %collective-permute-start.30) | collective-permute-done | bytes 393248 | tf_op jit(solution)/shard_map/ppermute | solution.py:15
  648.1 7.2 collective-permute-done.31
  655.4 4.0 copy.28
  659.5 1.8 broadcast.179
  661.3 98.2 %while.42 = (s32[]{:T(128)}, bf16[2,64,64,128]{3,2,1,0:T(8,128)(2,1)}, s32[2]{0:T(128)S(1)}, bf16[2,64,64,128]{3,2,1,0:T(8,128)(2,1)S(1)}, s32[2,8]{1,0:T(2,128)...) while((s32[]{:T(128)}, ...), condition=%wide.region_62.63_spmd.clone, body=%wide.region_61.62_spmd.clone.sunk | while | flops 102684736 | bytes 53919052 | solution.py:256
  689.1 3.3 maximum_maximum_fusion.6
  693.7 16.7 %bitcast_dynamic-update-slice_fusion.2 = bf16[2,64,64,128]{3,2,1,0:T(8,128)(2,1)} fusion(bf16[2,64,64,128]{3,2,1,0:T(8,128)(2,1)} %get-tuple-element.1782, s32[]{:T(128)} %get-tuple-element.1781, f32[]{:T(128)} %bitcast.632, f32[128]{0:T(128)S(1)} %get-tuple-element.1399, bf16[67,70,128]{2,1,0:T(8,128)(2,1)S(1)} %get-tuple-element.1430, ...), kind=kLoop, calls=%fused_computation.21.clone.1 | loop fusion | flops 88080384 | bytes 47310340 | tf_op jit(solution)/shard_map/while/body/jit(dynamic_update_index_in_dim)/dynamic_update_slice | solution.py:239
  738.2 3.3 maximum_maximum_fusion.6
  742.8 16.7 %bitcast_dynamic-update-slice_fusion.2 = bf16[2,64,64,128]{3,2,1,0:T(8,128)(2,1)} fusion(bf16[2,64,64,128]{3,2,1,0:T(8,128)(2,1)} %get-tuple-element.1782, s32[]{:T(128)} %get-tuple-element.1781, f32[]{:T(128)} %bitcast.632, f32[128]{0:T(128)S(1)} %get-tuple-element.1399, bf16[67,70,128]{2,1,0:T(8,128)(2,1)S(1)} %get-tuple-element.1430, ...), kind=kLoop, calls=%fused_computation.21.clone.1 | loop fusion | flops 88080384 | bytes 47310340 | tf_op jit(solution)/shard_map/while/body/jit(dynamic_update_index_in_dim)/dynamic_update_slice | solution.py:239
  759.5 2.7 all-reduce.7.cloned.1.call-done
  (498 shorter events, 95.4 us)
Async XLA Ops:
  7.2 652.3 %all-reduce.9.cloned.1.call-start = ((), (), s32[]{:S(2)}) async-start(), calls=%async_computation.1 | async-start | bytes 1048576 | tf_op jit(solution)/shard_map/psum | solution.py:258
  9.4 20.9 %collective-permute-start = (bf16[1,2,4,3,64,128]{5,4,3,2,1,0:T(8,128)(2,1)S(1)}, bf16[1,2,4,3,64,128]{5,4,3,2,1,0:T(8,128)(2,1)S(1)}, u32[]{:S(2)}, u32[]{:S(2)}) collective-permute-start(bf16[1,2,4,3,64,128]{5,4,3,2,1,0:T(8,128)(2,1)S(1)} %maximum_bitcast_fusion.1), channel_id=1, source_target_pairs={{0,32},{4,36},{8,40},{12,44},{16,48},{20,52},{24,56},{28,60},{32,6... | collective-permute-start | bytes 1179656 | tf_op jit(solution)/shard_map/ppermute | solution.py:15
  13.4 19.5 %collective-permute-start.1 = (bf16[1,2,4,3,64,128]{5,4,3,2,1,0:T(8,128)(2,1)S(1)}, bf16[1,2,4,3,64,128]{5,4,3,2,1,0:T(8,128)(2,1)S(1)}, u32[]{:S(2)}, u32[]{:S(2)}) collective-permute-start(bf16[1,2,4,3,64,128]{5,4,3,2,1,0:T(8,128)(2,1)S(1)} %maximum_bitcast_fusion.1), channel_id=1, source_target_pairs={{0,28},{4,32},{8,36},{12,40},{16,44},{20,48},{24,52},{28,56},{32,6... | collective-permute-start | bytes 1179656 | tf_op jit(solution)/shard_map/ppermute | solution.py:15
  17.4 31.4 %collective-permute-start.2 = (bf16[1,2,4,3,64,128]{5,4,3,2,1,0:T(8,128)(2,1)S(1)}, bf16[1,2,4,3,64,128]{5,4,3,2,1,0:T(8,128)(2,1)S(1)}, u32[]{:S(2)}, u32[]{:S(2)}) collective-permute-start(bf16[1,2,4,3,64,128]{5,4,3,2,1,0:T(8,128)(2,1)S(1)} %maximum_bitcast_fusion.1), channel_id=1, source_target_pairs={{0,24},{4,28},{8,32},{12,36},{16,40},{20,44},{24,48},{28,52},{32,5... | collective-permute-start | bytes 1179656 | tf_op jit(solution)/shard_map/ppermute | solution.py:15
  23.0 30.8 %collective-permute-start.3 = (bf16[1,2,4,3,64,128]{5,4,3,2,1,0:T(8,128)(2,1)S(1)}, bf16[1,2,4,3,64,128]{5,4,3,2,1,0:T(8,128)(2,1)S(1)}, u32[]{:S(2)}, u32[]{:S(2)}) collective-permute-start(bf16[1,2,4,3,64,128]{5,4,3,2,1,0:T(8,128)(2,1)S(1)} %maximum_bitcast_fusion.1), channel_id=1, source_target_pairs={{0,20},{4,24},{8,28},{12,32},{16,36},{20,40},{24,44},{28,48},{32,5... | collective-permute-start | bytes 1179656 | tf_op jit(solution)/shard_map/ppermute | solution.py:15
  25.1 30.7 %collective-permute-start.4 = (bf16[1,2,4,3,64,128]{5,4,3,2,1,0:T(8,128)(2,1)S(1)}, bf16[1,2,4,3,64,128]{5,4,3,2,1,0:T(8,128)(2,1)S(1)}, u32[]{:S(2)}, u32[]{:S(2)}) collective-permute-start(bf16[1,2,4,3,64,128]{5,4,3,2,1,0:T(8,128)(2,1)S(1)} %maximum_bitcast_fusion.1), channel_id=1, source_target_pairs={{0,16},{4,20},{8,24},{12,28},{16,32},{20,36},{24,40},{28,44},{32,4... | collective-permute-start | bytes 1179656 | tf_op jit(solution)/shard_map/ppermute | solution.py:15
  30.3 26.8 %collective-permute-start.5 = (bf16[1,2,4,3,64,128]{5,4,3,2,1,0:T(8,128)(2,1)S(1)}, bf16[1,2,4,3,64,128]{5,4,3,2,1,0:T(8,128)(2,1)S(1)}, u32[]{:S(2)}, u32[]{:S(2)}) collective-permute-start(bf16[1,2,4,3,64,128]{5,4,3,2,1,0:T(8,128)(2,1)S(1)} %maximum_bitcast_fusion.1), channel_id=1, source_target_pairs={{0,12},{4,16},{8,20},{12,24},{16,28},{20,32},{24,36},{28,40},{32,4... | collective-permute-start | bytes 1179656 | tf_op jit(solution)/shard_map/ppermute | solution.py:15
  32.9 25.5 %collective-permute-start.6 = (bf16[1,2,4,3,64,128]{5,4,3,2,1,0:T(8,128)(2,1)S(1)}, bf16[1,2,4,3,64,128]{5,4,3,2,1,0:T(8,128)(2,1)S(1)}, u32[]{:S(2)}, u32[]{:S(2)}) collective-permute-start(bf16[1,2,4,3,64,128]{5,4,3,2,1,0:T(8,128)(2,1)S(1)} %maximum_bitcast_fusion.1), channel_id=1, source_target_pairs={{0,8},{4,12},{8,16},{12,20},{16,24},{20,28},{24,32},{28,36},{32,40... | collective-permute-start | bytes 1179656 | tf_op jit(solution)/shard_map/ppermute | solution.py:15
  48.8 11.4 %collective-permute-start.7 = (bf16[1,2,4,3,64,128]{5,4,3,2,1,0:T(8,128)(2,1)S(1)}, bf16[1,2,4,3,64,128]{5,4,3,2,1,0:T(8,128)(2,1)S(1)}, u32[]{:S(2)}, u32[]{:S(2)}) collective-permute-start(bf16[1,2,4,3,64,128]{5,4,3,2,1,0:T(8,128)(2,1)S(1)} %maximum_bitcast_fusion.1), channel_id=1, source_target_pairs={{0,4},{4,8},{8,12},{12,16},{16,20},{20,24},{24,28},{28,32},{32,36}... | collective-permute-start | bytes 1179656 | tf_op jit(solution)/shard_map/ppermute | solution.py:15
  53.8 11.9 %collective-permute-start.8 = (bf16[1,2,4,3,64,128]{5,4,3,2,1,0:T(8,128)(2,1)S(1)}, bf16[1,2,4,3,64,128]{5,4,3,2,1,0:T(8,128)(2,1)S(1)}, u32[]{:S(2)}, u32[]{:S(2)}) collective-permute-start(bf16[1,2,4,3,64,128]{5,4,3,2,1,0:T(8,128)(2,1)S(1)} %maximum_bitcast_fusion.1), channel_id=1, source_target_pairs={{4,0},{8,4},{12,8},{16,12},{20,16},{24,20},{28,24},{32,28},{36,32}... | collective-permute-start | bytes 1179656 | tf_op jit(solution)/shard_map/ppermute | solution.py:15
  55.8 13.0 %collective-permute-start.9 = (bf16[1,2,4,3,64,128]{5,4,3,2,1,0:T(8,128)(2,1)S(1)}, bf16[1,2,4,3,64,128]{5,4,3,2,1,0:T(8,128)(2,1)S(1)}, u32[]{:S(2)}, u32[]{:S(2)}) collective-permute-start(bf16[1,2,4,3,64,128]{5,4,3,2,1,0:T(8,128)(2,1)S(1)} %maximum_bitcast_fusion.1), channel_id=1, source_target_pairs={{8,0},{12,4},{16,8},{20,12},{24,16},{28,20},{32,24},{36,28},{40,32... | collective-permute-start | bytes 1179656 | tf_op jit(solution)/shard_map/ppermute | solution.py:15
  57.2 14.5 %collective-permute-start.10 = (bf16[1,2,4,3,64,128]{5,4,3,2,1,0:T(8,128)(2,1)S(1)}, bf16[1,2,4,3,64,128]{5,4,3,2,1,0:T(8,128)(2,1)S(1)}, u32[]{:S(2)}, u32[]{:S(2)}) collective-permute-start(bf16[1,2,4,3,64,128]{5,4,3,2,1,0:T(8,128)(2,1)S(1)} %maximum_bitcast_fusion.1), channel_id=1, source_target_pairs={{12,0},{16,4},{20,8},{24,12},{28,16},{32,20},{36,24},{40,28},{44,3... | collective-permute-start | bytes 1179656 | tf_op jit(solution)/shard_map/ppermute | solution.py:15
  58.5 19.3 %collective-permute-start.11 = (bf16[1,2,4,3,64,128]{5,4,3,2,1,0:T(8,128)(2,1)S(1)}, bf16[1,2,4,3,64,128]{5,4,3,2,1,0:T(8,128)(2,1)S(1)}, u32[]{:S(2)}, u32[]{:S(2)}) collective-permute-start(bf16[1,2,4,3,64,128]{5,4,3,2,1,0:T(8,128)(2,1)S(1)} %maximum_bitcast_fusion.1), channel_id=1, source_target_pairs={{16,0},{20,4},{24,8},{28,12},{32,16},{36,20},{40,24},{44,28},{48,3... | collective-permute-start | bytes 1179656 | tf_op jit(solution)/shard_map/ppermute | solution.py:15
  60.2 28.4 %collective-permute-start.12 = (bf16[1,2,4,3,64,128]{5,4,3,2,1,0:T(8,128)(2,1)S(1)}, bf16[1,2,4,3,64,128]{5,4,3,2,1,0:T(8,128)(2,1)S(1)}, u32[]{:S(2)}, u32[]{:S(2)}) collective-permute-start(bf16[1,2,4,3,64,128]{5,4,3,2,1,0:T(8,128)(2,1)S(1)} %maximum_bitcast_fusion.1), channel_id=1, source_target_pairs={{20,0},{24,4},{28,8},{32,12},{36,16},{40,20},{44,24},{48,28},{52,3... | collective-permute-start | bytes 1179656 | tf_op jit(solution)/shard_map/ppermute | solution.py:15
  65.7 31.3 %collective-permute-start.13 = (bf16[1,2,4,3,64,128]{5,4,3,2,1,0:T(8,128)(2,1)S(1)}, bf16[1,2,4,3,64,128]{5,4,3,2,1,0:T(8,128)(2,1)S(1)}, u32[]{:S(2)}, u32[]{:S(2)}) collective-permute-start(bf16[1,2,4,3,64,128]{5,4,3,2,1,0:T(8,128)(2,1)S(1)} %maximum_bitcast_fusion.1), channel_id=1, source_target_pairs={{24,0},{28,4},{32,8},{36,12},{40,16},{44,20},{48,24},{52,28},{56,3... | collective-permute-start | bytes 1179656 | tf_op jit(solution)/shard_map/ppermute | solution.py:15
  68.8 50.5 %collective-permute-start.14 = (bf16[1,2,4,3,64,128]{5,4,3,2,1,0:T(8,128)(2,1)S(1)}, bf16[1,2,4,3,64,128]{5,4,3,2,1,0:T(8,128)(2,1)S(1)}, u32[]{:S(2)}, u32[]{:S(2)}) collective-permute-start(bf16[1,2,4,3,64,128]{5,4,3,2,1,0:T(8,128)(2,1)S(1)} %maximum_bitcast_fusion.1), channel_id=1, source_target_pairs={{28,0},{32,4},{36,8},{40,12},{44,16},{48,20},{52,24},{56,28},{60,3... | collective-permute-start | bytes 1179656 | tf_op jit(solution)/shard_map/ppermute | solution.py:15
  71.6 49.3 %collective-permute-start.15 = (bf16[1,2,4,3,64,128]{5,4,3,2,1,0:T(8,128)(2,1)S(1)}, bf16[1,2,4,3,64,128]{5,4,3,2,1,0:T(8,128)(2,1)S(1)}, u32[]{:S(2)}, u32[]{:S(2)}) collective-permute-start(bf16[1,2,4,3,64,128]{5,4,3,2,1,0:T(8,128)(2,1)S(1)} %maximum_bitcast_fusion.1), channel_id=1, source_target_pairs={{32,0},{36,4},{40,8},{44,12},{48,16},{52,20},{56,24},{60,28},{64,3... | collective-permute-start | bytes 1179656 | tf_op jit(solution)/shard_map/ppermute | solution.py:15
  145.3 20.7 %copy-start.73 = (s32[2]{0:T(128)}, s32[2]{0:T(128)S(1)}, u32[]{:S(2)}) copy-start(s32[2]{0:T(128)S(1)} %get-tuple-element.1737) | copy-start | bytes 28 | tf_op jit(solution)/shard_map/while
  165.9 11.4 %copy-start.12 = (bf16[64,3,128]{2,1,0:T(4,128)(2,1)}, bf16[64,3,128]{2,1,0:T(4,128)(2,1)S(1)}, u32[]{:S(2)}) copy-start(bf16[64,3,128]{2,1,0:T(4,128)(2,1)S(1)} %get-tuple-element.1523) | copy-start | bytes 147460 | tf_op jit(solution)/shard_map/while
  166.0 11.4 %copy-start.13 = (bf16[64,3,128]{2,1,0:T(4,128)(2,1)}, bf16[64,3,128]{2,1,0:T(4,128)(2,1)S(1)}, u32[]{:S(2)}) copy-start(bf16[64,3,128]{2,1,0:T(4,128)(2,1)S(1)} %get-tuple-element.1524) | copy-start | bytes 147460 | tf_op jit(solution)/shard_map/while
  174.1 19.6 %copy-start.3 = (bf16[64,64,128]{2,1,0:T(8,128)(2,1)}, bf16[64,64,128]{2,1,0:T(8,128)(2,1)S(1)}, u32[]{:S(2)}) copy-start(bf16[64,64,128]{2,1,0:T(8,128)(2,1)S(1)} %fusion.229) | copy-start | bytes 3145732 | tf_op jit(solution)/shard_map/while
  203.5 20.7 %copy-start.2 = (bf16[4096,512]{1,0:T(8,128)(2,1)}, bf16[4096,512]{1,0:T(8,128)(2,1)S(1)}, u32[]{:S(2)}) copy-start(bf16[4096,512]{1,0:T(8,128)(2,1)S(1)} %get-tuple-element.1650) | copy-start | bytes 12582916 | tf_op jit(solution)/shard_map/while
  214.1 9.7 %copy-start.10 = (bf16[2,64,64,128]{3,2,1,0:T(8,128)(2,1)S(1)}, bf16[2,64,64,128]{3,2,1,0:T(8,128)(2,1)}, u32[]{:S(2)}) copy-start(bf16[2,64,64,128]{3,2,1,0:T(8,128)(2,1)} %get-tuple-element.1700) | copy-start | bytes 6291460 | tf_op jit(solution)/shard_map/while
  237.2 8.8 %copy-start.27 = (f32[128]{0:T(128)S(1)}, f32[128]{0:T(128)}, u32[]{:S(2)}) copy-start(f32[128]{0:T(128)} %get-tuple-element.1628) | copy-start | bytes 1540 | tf_op jit(solution)/shard_map/while
  237.2 8.8 %copy-start.28 = (f32[128]{0:T(128)S(1)}, f32[128]{0:T(128)}, u32[]{:S(2)}) copy-start(f32[128]{0:T(128)} %get-tuple-element.1627) | copy-start | bytes 1540 | tf_op jit(solution)/shard_map/while
  237.2 8.8 %copy-start.29 = (f32[128]{0:T(128)S(1)}, f32[128]{0:T(128)}, u32[]{:S(2)}) copy-start(f32[128]{0:T(128)} %get-tuple-element.1626) | copy-start | bytes 1540 | tf_op jit(solution)/shard_map/while
  237.2 8.7 %copy-start.30 = (f32[128]{0:T(128)S(1)}, f32[128]{0:T(128)}, u32[]{:S(2)}) copy-start(f32[128]{0:T(128)} %get-tuple-element.1625) | copy-start | bytes 1540 | tf_op jit(solution)/shard_map/while
  247.4 7.3 copy-start.22
  247.5 7.3 copy-start.8
  259.4 20.7 %copy-start.73 = (s32[2]{0:T(128)}, s32[2]{0:T(128)S(1)}, u32[]{:S(2)}) copy-start(s32[2]{0:T(128)S(1)} %get-tuple-element.1737) | copy-start | bytes 28 | tf_op jit(solution)/shard_map/while
  280.0 11.4 %copy-start.12 = (bf16[64,3,128]{2,1,0:T(4,128)(2,1)}, bf16[64,3,128]{2,1,0:T(4,128)(2,1)S(1)}, u32[]{:S(2)}) copy-start(bf16[64,3,128]{2,1,0:T(4,128)(2,1)S(1)} %get-tuple-element.1523) | copy-start | bytes 147460 | tf_op jit(solution)/shard_map/while
  280.0 11.4 %copy-start.13 = (bf16[64,3,128]{2,1,0:T(4,128)(2,1)}, bf16[64,3,128]{2,1,0:T(4,128)(2,1)S(1)}, u32[]{:S(2)}) copy-start(bf16[64,3,128]{2,1,0:T(4,128)(2,1)S(1)} %get-tuple-element.1524) | copy-start | bytes 147460 | tf_op jit(solution)/shard_map/while
  288.1 19.6 %copy-start.3 = (bf16[64,64,128]{2,1,0:T(8,128)(2,1)}, bf16[64,64,128]{2,1,0:T(8,128)(2,1)S(1)}, u32[]{:S(2)}) copy-start(bf16[64,64,128]{2,1,0:T(8,128)(2,1)S(1)} %fusion.229) | copy-start | bytes 3145732 | tf_op jit(solution)/shard_map/while
  317.5 20.7 %copy-start.2 = (bf16[4096,512]{1,0:T(8,128)(2,1)}, bf16[4096,512]{1,0:T(8,128)(2,1)S(1)}, u32[]{:S(2)}) copy-start(bf16[4096,512]{1,0:T(8,128)(2,1)S(1)} %get-tuple-element.1650) | copy-start | bytes 12582916 | tf_op jit(solution)/shard_map/while
  328.1 9.7 %copy-start.10 = (bf16[2,64,64,128]{3,2,1,0:T(8,128)(2,1)S(1)}, bf16[2,64,64,128]{3,2,1,0:T(8,128)(2,1)}, u32[]{:S(2)}) copy-start(bf16[2,64,64,128]{3,2,1,0:T(8,128)(2,1)} %get-tuple-element.1700) | copy-start | bytes 6291460 | tf_op jit(solution)/shard_map/while
  351.3 8.8 %copy-start.27 = (f32[128]{0:T(128)S(1)}, f32[128]{0:T(128)}, u32[]{:S(2)}) copy-start(f32[128]{0:T(128)} %get-tuple-element.1628) | copy-start | bytes 1540 | tf_op jit(solution)/shard_map/while
  351.3 8.8 %copy-start.28 = (f32[128]{0:T(128)S(1)}, f32[128]{0:T(128)}, u32[]{:S(2)}) copy-start(f32[128]{0:T(128)} %get-tuple-element.1627) | copy-start | bytes 1540 | tf_op jit(solution)/shard_map/while
  351.3 8.8 %copy-start.29 = (f32[128]{0:T(128)S(1)}, f32[128]{0:T(128)}, u32[]{:S(2)}) copy-start(f32[128]{0:T(128)} %get-tuple-element.1626) | copy-start | bytes 1540 | tf_op jit(solution)/shard_map/while
  351.3 8.7 %copy-start.30 = (f32[128]{0:T(128)S(1)}, f32[128]{0:T(128)}, u32[]{:S(2)}) copy-start(f32[128]{0:T(128)} %get-tuple-element.1625) | copy-start | bytes 1540 | tf_op jit(solution)/shard_map/while
  361.5 7.3 copy-start.8
  373.6 22.0 %copy-start.21 = (f32[7,7,128]{2,1,0:T(8,128)S(1)}, f32[7,7,128]{2,1,0:T(8,128)}, u32[]{:S(2)}) copy-start(f32[7,7,128]{2,1,0:T(8,128)} %get-tuple-element.2229) | copy-start | bytes 75268
  373.6 21.9 %copy-start.24 = (f32[512]{0:T(512)S(1)}, f32[512]{0:T(512)}, u32[]{:S(2)}) copy-start(f32[512]{0:T(512)} %get-tuple-element.2234) | copy-start | bytes 6148
  373.6 21.9 %copy-start.48 = (f32[128]{0:T(128)S(1)}, f32[128]{0:T(128)}, u32[]{:S(2)}) copy-start(f32[128]{0:T(128)} %get-tuple-element.2237) | copy-start | bytes 1540
  373.6 21.9 %copy-start.51 = (f32[128]{0:T(128)S(1)}, f32[128]{0:T(128)}, u32[]{:S(2)}) copy-start(f32[128]{0:T(128)} %get-tuple-element.2230) | copy-start | bytes 1540
  373.7 21.9 %copy-start.54 = (f32[128]{0:T(128)S(1)}, f32[128]{0:T(128)}, u32[]{:S(2)}) copy-start(f32[128]{0:T(128)} %get-tuple-element.2231) | copy-start | bytes 1540
  373.7 21.9 %copy-start.57 = (f32[128]{0:T(128)S(1)}, f32[128]{0:T(128)}, u32[]{:S(2)}) copy-start(f32[128]{0:T(128)} %get-tuple-element.2232) | copy-start | bytes 1540
  373.7 21.9 %copy-start.60 = (f32[128]{0:T(128)S(1)}, f32[128]{0:T(128)}, u32[]{:S(2)}) copy-start(f32[128]{0:T(128)} %get-tuple-element.2236) | copy-start | bytes 1540
  376.5 201.6 %collective-permute-start.23 = (bf16[1,2,4,3,64,128]{5,3,4,1,0,2:T(4,128)(2,1)S(1)}, bf16[1,2,4,3,64,128]{5,3,4,1,0,2:T(4,128)(2,1)S(1)}, u32[]{:S(2)}, u32[]{:S(2)}) collective-permute-start(bf16[1,2,4,3,64,128]{5,3,4,1,0,2:T(4,128)(2,1)S(1)} %maximum_bitcast_fusion), channel_id=1, source_target_pairs={{0,4},{4,8},{8,12},{12,16},{16,20},{20,24},{24,28},{28,32},{32,36}... | collective-permute-start | bytes 1179656 | tf_op jit(solution)/shard_map/ppermute | solution.py:15
  383.0 196.6 %collective-permute-start.24 = (bf16[1,2,4,3,64,128]{5,3,4,1,0,2:T(4,128)(2,1)S(1)}, bf16[1,2,4,3,64,128]{5,3,4,1,0,2:T(4,128)(2,1)S(1)}, u32[]{:S(2)}, u32[]{:S(2)}) collective-permute-start(bf16[1,2,4,3,64,128]{5,3,4,1,0,2:T(4,128)(2,1)S(1)} %maximum_bitcast_fusion), channel_id=1, source_target_pairs={{4,0},{8,4},{12,8},{16,12},{20,16},{24,20},{28,24},{32,28},{36,32}... | collective-permute-start | bytes 1179656 | tf_op jit(solution)/shard_map/ppermute | solution.py:15
  385.0 149.1 %collective-permute-start.16 = (bf16[1,2,4,3,64,128]{5,3,4,1,0,2:T(4,128)(2,1)S(1)}, bf16[1,2,4,3,64,128]{5,3,4,1,0,2:T(4,128)(2,1)S(1)}, u32[]{:S(2)}, u32[]{:S(2)}) collective-permute-start(bf16[1,2,4,3,64,128]{5,3,4,1,0,2:T(4,128)(2,1)S(1)} %maximum_bitcast_fusion), channel_id=1, source_target_pairs={{0,32},{4,36},{8,40},{12,44},{16,48},{20,52},{24,56},{28,60},{32,6... | collective-permute-start | bytes 1179656 | tf_op jit(solution)/shard_map/ppermute | solution.py:15
  388.3 147.2 %collective-permute-start.17 = (bf16[1,2,4,3,64,128]{5,3,4,1,0,2:T(4,128)(2,1)S(1)}, bf16[1,2,4,3,64,128]{5,3,4,1,0,2:T(4,128)(2,1)S(1)}, u32[]{:S(2)}, u32[]{:S(2)}) collective-permute-start(bf16[1,2,4,3,64,128]{5,3,4,1,0,2:T(4,128)(2,1)S(1)} %maximum_bitcast_fusion), channel_id=1, source_target_pairs={{0,28},{4,32},{8,36},{12,40},{16,44},{20,48},{24,52},{28,56},{32,6... | collective-permute-start | bytes 1179656 | tf_op jit(solution)/shard_map/ppermute | solution.py:15
  394.2 142.7 %collective-permute-start.18 = (bf16[1,2,4,3,64,128]{5,3,4,1,0,2:T(4,128)(2,1)S(1)}, bf16[1,2,4,3,64,128]{5,3,4,1,0,2:T(4,128)(2,1)S(1)}, u32[]{:S(2)}, u32[]{:S(2)}) collective-permute-start(bf16[1,2,4,3,64,128]{5,3,4,1,0,2:T(4,128)(2,1)S(1)} %maximum_bitcast_fusion), channel_id=1, source_target_pairs={{0,24},{4,28},{8,32},{12,36},{16,40},{20,44},{24,48},{28,52},{32,5... | collective-permute-start | bytes 1179656 | tf_op jit(solution)/shard_map/ppermute | solution.py:15
  533.0 229.2 %all-reduce.7.cloned.1.call-start = ((), (), s32[]{:S(2)}) async-start(), calls=%async_computation | async-start | bytes 1048576 | tf_op jit(solution)/shard_map/psum | solution.py:257
  534.1 32.8 %collective-permute-start.19 = (bf16[1,2,4,3,64,128]{5,3,4,1,0,2:T(4,128)(2,1)S(1)}, bf16[1,2,4,3,64,128]{5,3,4,1,0,2:T(4,128)(2,1)S(1)}, u32[]{:S(2)}, u32[]{:S(2)}) collective-permute-start(bf16[1,2,4,3,64,128]{5,3,4,1,0,2:T(4,128)(2,1)S(1)} %maximum_bitcast_fusion), channel_id=1, source_target_pairs={{0,20},{4,24},{8,28},{12,32},{16,36},{20,40},{24,44},{28,48},{32,5... | collective-permute-start | bytes 1179656 | tf_op jit(solution)/shard_map/ppermute | solution.py:15
  535.5 32.8 %collective-permute-start.20 = (bf16[1,2,4,3,64,128]{5,3,4,1,0,2:T(4,128)(2,1)S(1)}, bf16[1,2,4,3,64,128]{5,3,4,1,0,2:T(4,128)(2,1)S(1)}, u32[]{:S(2)}, u32[]{:S(2)}) collective-permute-start(bf16[1,2,4,3,64,128]{5,3,4,1,0,2:T(4,128)(2,1)S(1)} %maximum_bitcast_fusion), channel_id=1, source_target_pairs={{0,16},{4,20},{8,24},{12,28},{16,32},{20,36},{24,40},{28,44},{32,4... | collective-permute-start | bytes 1179656 | tf_op jit(solution)/shard_map/ppermute | solution.py:15
  537.0 32.8 %collective-permute-start.21 = (bf16[1,2,4,3,64,128]{5,3,4,1,0,2:T(4,128)(2,1)S(1)}, bf16[1,2,4,3,64,128]{5,3,4,1,0,2:T(4,128)(2,1)S(1)}, u32[]{:S(2)}, u32[]{:S(2)}) collective-permute-start(bf16[1,2,4,3,64,128]{5,3,4,1,0,2:T(4,128)(2,1)S(1)} %maximum_bitcast_fusion), channel_id=1, source_target_pairs={{0,12},{4,16},{8,20},{12,24},{16,28},{20,32},{24,36},{28,40},{32,4... | collective-permute-start | bytes 1179656 | tf_op jit(solution)/shard_map/ppermute | solution.py:15
  566.9 9.8 %collective-permute-start.22 = (bf16[1,2,4,3,64,128]{5,3,4,1,0,2:T(4,128)(2,1)S(1)}, bf16[1,2,4,3,64,128]{5,3,4,1,0,2:T(4,128)(2,1)S(1)}, u32[]{:S(2)}, u32[]{:S(2)}) collective-permute-start(bf16[1,2,4,3,64,128]{5,3,4,1,0,2:T(4,128)(2,1)S(1)} %maximum_bitcast_fusion), channel_id=1, source_target_pairs={{0,8},{4,12},{8,16},{12,20},{16,24},{20,28},{24,32},{28,36},{32,40... | collective-permute-start | bytes 1179656 | tf_op jit(solution)/shard_map/ppermute | solution.py:15
  568.3 13.5 %collective-permute-start.25 = (bf16[1,2,4,3,64,128]{5,3,4,1,0,2:T(4,128)(2,1)S(1)}, bf16[1,2,4,3,64,128]{5,3,4,1,0,2:T(4,128)(2,1)S(1)}, u32[]{:S(2)}, u32[]{:S(2)}) collective-permute-start(bf16[1,2,4,3,64,128]{5,3,4,1,0,2:T(4,128)(2,1)S(1)} %maximum_bitcast_fusion), channel_id=1, source_target_pairs={{8,0},{12,4},{16,8},{20,12},{24,16},{28,20},{32,24},{36,28},{40,32... | collective-permute-start | bytes 1179656 | tf_op jit(solution)/shard_map/ppermute | solution.py:15
  569.8 20.7 %collective-permute-start.26 = (bf16[1,2,4,3,64,128]{5,3,4,1,0,2:T(4,128)(2,1)S(1)}, bf16[1,2,4,3,64,128]{5,3,4,1,0,2:T(4,128)(2,1)S(1)}, u32[]{:S(2)}, u32[]{:S(2)}) collective-permute-start(bf16[1,2,4,3,64,128]{5,3,4,1,0,2:T(4,128)(2,1)S(1)} %maximum_bitcast_fusion), channel_id=1, source_target_pairs={{12,0},{16,4},{20,8},{24,12},{28,16},{32,20},{36,24},{40,28},{44,3... | collective-permute-start | bytes 1179656 | tf_op jit(solution)/shard_map/ppermute | solution.py:15
  576.7 38.8 %collective-permute-start.27 = (bf16[1,2,4,3,64,128]{5,3,4,1,0,2:T(4,128)(2,1)S(1)}, bf16[1,2,4,3,64,128]{5,3,4,1,0,2:T(4,128)(2,1)S(1)}, u32[]{:S(2)}, u32[]{:S(2)}) collective-permute-start(bf16[1,2,4,3,64,128]{5,3,4,1,0,2:T(4,128)(2,1)S(1)} %maximum_bitcast_fusion), channel_id=1, source_target_pairs={{16,0},{20,4},{24,8},{28,12},{32,16},{36,20},{40,24},{44,28},{48,3... | collective-permute-start | bytes 1179656 | tf_op jit(solution)/shard_map/ppermute | solution.py:15
  578.1 37.5 %collective-permute-start.28 = (bf16[1,2,4,3,64,128]{5,3,4,1,0,2:T(4,128)(2,1)S(1)}, bf16[1,2,4,3,64,128]{5,3,4,1,0,2:T(4,128)(2,1)S(1)}, u32[]{:S(2)}, u32[]{:S(2)}) collective-permute-start(bf16[1,2,4,3,64,128]{5,3,4,1,0,2:T(4,128)(2,1)S(1)} %maximum_bitcast_fusion), channel_id=1, source_target_pairs={{20,0},{24,4},{28,8},{32,12},{36,16},{40,20},{44,24},{48,28},{52,3... | collective-permute-start | bytes 1179656 | tf_op jit(solution)/shard_map/ppermute | solution.py:15
  579.6 36.1 %collective-permute-start.29 = (bf16[1,2,4,3,64,128]{5,3,4,1,0,2:T(4,128)(2,1)S(1)}, bf16[1,2,4,3,64,128]{5,3,4,1,0,2:T(4,128)(2,1)S(1)}, u32[]{:S(2)}, u32[]{:S(2)}) collective-permute-start(bf16[1,2,4,3,64,128]{5,3,4,1,0,2:T(4,128)(2,1)S(1)} %maximum_bitcast_fusion), channel_id=1, source_target_pairs={{24,0},{28,4},{32,8},{36,12},{40,16},{44,20},{48,24},{52,28},{56,3... | collective-permute-start | bytes 1179656 | tf_op jit(solution)/shard_map/ppermute | solution.py:15
  581.8 66.2 %collective-permute-start.30 = (bf16[1,2,4,3,64,128]{5,3,4,1,0,2:T(4,128)(2,1)S(1)}, bf16[1,2,4,3,64,128]{5,3,4,1,0,2:T(4,128)(2,1)S(1)}, u32[]{:S(2)}, u32[]{:S(2)}) collective-permute-start(bf16[1,2,4,3,64,128]{5,3,4,1,0,2:T(4,128)(2,1)S(1)} %maximum_bitcast_fusion), channel_id=1, source_target_pairs={{28,0},{32,4},{36,8},{40,12},{44,16},{48,20},{52,24},{56,28},{60,3... | collective-permute-start | bytes 1179656 | tf_op jit(solution)/shard_map/ppermute | solution.py:15
  590.4 64.8 %collective-permute-start.31 = (bf16[1,2,4,3,64,128]{5,3,4,1,0,2:T(4,128)(2,1)S(1)}, bf16[1,2,4,3,64,128]{5,3,4,1,0,2:T(4,128)(2,1)S(1)}, u32[]{:S(2)}, u32[]{:S(2)}) collective-permute-start(bf16[1,2,4,3,64,128]{5,3,4,1,0,2:T(4,128)(2,1)S(1)} %maximum_bitcast_fusion), channel_id=1, source_target_pairs={{32,0},{36,4},{40,8},{44,12},{48,16},{52,20},{56,24},{60,28},{64,3... | collective-permute-start | bytes 1179656 | tf_op jit(solution)/shard_map/ppermute | solution.py:15
  (100 other events, 391.9 us)
Sparse Core Ops, SparseCore 0:
  533.1 40.6 all-reduce.8
  659.6 102.5 all-reduce.6
